TPU v7x, 128 devices: a whole 4x4x4 slice. The times are simulated.
128 devices in a mesh: mem: 8 (over z, core), lat: 16 (over y, x).
Axes of the slice: x: 4, y: 4, z: 4, core: 2. Of those that a mesh axis runs over, the one named last changes fastest.
Arguments:
- perturbations: bfloat16 [256, 3, 384, 1280], P('mem', None, 'lat'), may hold values from -0.375 to 0.375
- control: float32 [256, 96, 320], P('mem', 'lat'), may hold values from -6 to 6
- innovations: float32 [3, 384, 1280], P(None, 'lat'), may hold values from -6 to 6
- thresholds: float32 [3], replicated, may hold values from 0.4 to 1.5
Outputs:
- weights: float32 [256, 96, 320], P('mem', 'lat')
- increment: float32 [3, 384, 1280], P(None, 'lat', 'mem')
All inputs are finite; a program needn't handle non-finite values.
Results may differ from a plain program's by a relative error of at most 0.0003.
Values sent between devices are 32-bit elements; how exact they have to be, the bound alone decides.
A program may use at most 64 MiB of HBM per device.

v0:
```python
import jax
import jax.numpy as jnp
from jax import lax
from jax.sharding import PartitionSpec as P

RATIO = 4
HALF = 5
STEPS = 2


def with_halo(cells, sides, width):
    for axis, dim in sides:
        count = lax.axis_size(axis)
        ends = count - 1
        head = lax.slice_in_dim(cells, 0, width, axis=dim)
        tail = lax.slice_in_dim(cells, cells.shape[dim] - width, cells.shape[dim], axis=dim)
        cells = jnp.concatenate(
            [
                lax.ppermute(tail, axis, [(i, (i + 1) % count) for i in range(ends)]),
                cells,
                lax.ppermute(head, axis, [((i + 1) % count, i) for i in range(ends)]),
            ],
            axis=dim,
        )
    return cells


def tent(fine_pos, coarse_pos, period):
    distance = fine_pos[:, None] + 0.5 - RATIO * coarse_pos[None, :] - RATIO / 2
    if period:
        distance = jnp.mod(distance + period / 2, period) - period / 2
    return jnp.maximum(0.0, 1.0 - jnp.abs(distance) / RATIO)


def smoother(rows, cols, offset):
    distance = jnp.abs(
        jnp.arange(cols, dtype=jnp.float32)[None, :]
        - jnp.arange(rows, dtype=jnp.float32)[:, None]
        - offset
    )
    return jnp.where(distance <= HALF, (1.0 - distance / (HALF + 1)) / 2, 0.0)


def per_device(perturbations, control, innovations, thresholds):
    highest = lax.Precision.HIGHEST
    members, coarse_rows, coarse_cols = control.shape
    fine_rows = RATIO * coarse_rows
    fine_cols = RATIO * coarse_cols
    fine_edge = RATIO // 2
    share_cols = fine_cols // lax.axis_size("mem")
    rows_f = jnp.arange(fine_rows, dtype=jnp.float32)
    lat_up = tent(rows_f, jnp.arange(coarse_rows + 2, dtype=jnp.float32) - 1.0, 0)
    lat_down = tent(
        jnp.arange(fine_rows + 2 * fine_edge, dtype=jnp.float32) - fine_edge,
        jnp.arange(coarse_rows, dtype=jnp.float32),
        0,
    ).T
    lon_up = tent(
        jnp.arange(fine_cols, dtype=jnp.float32),
        jnp.arange(coarse_cols, dtype=jnp.float32),
        fine_cols,
    ).T
    smooth_band = smoother(coarse_rows, coarse_rows + 2 * HALF, HALF)

    def forward(weights):
        padded = with_halo(weights, (("lat", 1),), HALF)
        smoothed = jnp.einsum("jq,mqc->mjc", smooth_band, padded, precision=highest)
        widened = with_halo(smoothed, (("lat", 1),), 1)
        rowwise = jnp.einsum("iq,mqc->mic", lat_up, widened, precision=highest)
        refined = jnp.dot(
            rowwise.reshape(members * fine_rows, coarse_cols), lon_up, precision=highest
        )
        refined = refined.reshape(members, fine_rows, fine_cols)
        return jnp.sum(perturbations.astype(jnp.float32) * refined[:, None], axis=0)

    def combine_members(partial_value):
        return lax.psum(partial_value, "mem")

    limit = thresholds[:, None, None]
    weights = control
    increment = combine_members(forward(control))
    for iteration in range(STEPS):
        misfit = jnp.clip(increment - innovations, -limit, limit)
        weighted = jnp.sum(perturbations.astype(jnp.float32) * misfit[None], axis=1)
        columns = jnp.einsum("mif,cf->mic", weighted, lon_up, precision=highest)
        adjoint_padded = with_halo(columns, (("lat", 1),), fine_edge)
        coarse = jnp.einsum("ji,mic->mjc", lat_down, adjoint_padded, precision=highest)
        adjoint_widened = with_halo(coarse, (("lat", 1),), HALF)
        gradient = weights + jnp.einsum(
            "jq,mqc->mjc", smooth_band, adjoint_widened, precision=highest
        )
        grad_sq = lax.psum(jnp.sum(gradient * gradient), ("mem", "lat"))
        image = combine_members(forward(gradient))
        image_sq = lax.psum(jnp.sum(image * image), "lat")
        step_len = grad_sq / (grad_sq + image_sq)
        weights = weights - step_len * gradient
        increment = increment - step_len * image
    result = lax.dynamic_slice_in_dim(increment, lax.axis_index("mem") * share_cols, share_cols, 2)
    return (weights, result)


def solution(mesh):
    return jax.shard_map(
        per_device,
        mesh=mesh,
        in_specs=(P("mem", None, "lat", None), P("mem", "lat", None), P(None, "lat", None), P()),
        out_specs=(P("mem", "lat", None), P(None, "lat", "mem")),
        check_vma=False,
    )
```

profile of v0, /device:TPU:0, one launch (start us, length us, event | category | flops | bytes accessed | tf_op | source)
XLA Modules:
  0.0 608.4 jit_solution(18204806061772033383)
XLA Ops:
  7.2 1.1 copy.10
  8.4 1.3 collective-permute-start.1
  9.7 4.6 collective-permute-start
  14.3 6.7 %collective-permute-done.1 = f32[32,5,320]{2,1,0:T(8,128)S(1)} collective-permute-done((f32[32,5,320]{2,1,0:T(8,128)S(1)}, f32[32,5,320]{2,1,0:T(8,128)S(1)}, u32[]{:S(2)}, u32[]{:S(2)}) %collective-permute-start.1) | collective-permute-done | bytes 204832 | tf_op jit(solution)/shard_map/ppermute | solution.py:21
  21.0 1.2 collective-permute-done
  23.0 1.4 collective-permute-start.3
  24.4 5.0 collective-permute-start.2
  29.6 1.6 collective-permute-done.2
  31.2 1.1 convolution_bitcast_fusion.2
  32.3 7.7 %fusion.34 = f32[32,24,1280]{2,1,0:T(8,128)S(1)} fusion(f32[32,24,320]{2,1,0:T(8,128)S(1)} %convolution_bitcast_fusion.2, f32[320]{0:T(512)S(1)} %iota_multiply_fusion, f32[1280]{0:T(1024)S(1)} %iota_add_fusion), kind=kOutput, calls=%fused_computation.37 | convolution fusion | flops 3780198400 | bytes 4921600 | tf_op jit(solution)/shard_map/dot_general | solution.py:70
  40.1 1.9 fusion
  42.6 68.1 %all-reduce.4.cloned.1.call-done = f32[3,24,1280]{2,1,0:T(8,128)} async-done(((f32[3,24,1280]{2,1,0:T(8,128)}), f32[3,24,1280]{2,1,0:T(8,128)}) %all-reduce.4.cloned.1.call-update) | async-done | bytes 368656 | tf_op jit(solution)/shard_map/psum | solution.py:77
  111.8 4.5 fusion.1
  116.3 7.4 %fusion.32 = f32[32,24,320]{2,1,0:T(8,128)S(1)} fusion(f32[32,24,1280]{2,1,0:T(8,128)S(1)} %fusion.1, f32[320]{0:T(512)S(1)} %iota_multiply_fusion, f32[1280]{0:T(1024)S(1)} %iota_add_fusion), kind=kOutput, calls=%fused_computation.36 | convolution fusion | flops 3780198400 | bytes 4921600 | tf_op jit(solution)/shard_map/mif,cf->mic/dot_general | solution.py:85
  123.8 1.3 collective-permute-start.5
  125.1 4.6 collective-permute-start.4
  130.4 1.5 collective-permute-done.4
  131.9 1.3 fusion.39
  133.3 1.3 collective-permute-start.7
  134.6 5.0 collective-permute-start.6
  139.5 3.8 collective-permute-done.7
  143.3 1.5 collective-permute-done.6
  144.8 1.4 multiply_reduce_fusion.1
  146.3 1.3 collective-permute-start.9
  147.6 5.0 collective-permute-start.8
  152.6 3.8 collective-permute-done.9
  156.4 1.5 collective-permute-done.8
  158.7 1.4 collective-permute-start.11
  160.1 5.2 collective-permute-start.10
  165.3 1.5 collective-permute-done.10
  166.9 1.1 convolution_bitcast_fusion.1
  168.0 7.7 %fusion.30 = f32[32,24,1280]{2,1,0:T(8,128)S(1)} fusion(f32[32,24,320]{2,1,0:T(8,128)S(1)} %convolution_bitcast_fusion.1, f32[320]{0:T(512)S(1)} %iota_multiply_fusion, f32[1280]{0:T(1024)S(1)} %iota_add_fusion), kind=kOutput, calls=%fused_computation.35 | convolution fusion | flops 3780198400 | bytes 4921600 | tf_op jit(solution)/shard_map/dot_general | solution.py:70
  175.7 1.9 fusion.2
  177.8 73.0 %all-reduce.6.cloned.1.call-done = f32[3,24,1280]{2,1,0:T(8,128)} async-done(((f32[3,24,1280]{2,1,0:T(8,128)}), f32[3,24,1280]{2,1,0:T(8,128)}) %all-reduce.6.cloned.1.call-update) | async-done | bytes 368656 | tf_op jit(solution)/shard_map/psum | solution.py:77
  250.7 1.7 multiply_reduce_fusion.3
  252.4 64.9 %psum.50 = f32[]{:T(128)} all-reduce(f32[]{:T(128)} %get-tuple-element.26), channel_id=1, replica_groups=mesh['mem'=8,'lat'=16] {'mem','lat'}, use_global_device_ids=true, to_apply=%region_4.5 | all-reduce | flops 1 | bytes 8 | tf_op jit(solution)/shard_map/psum | solution.py:92
  317.3 38.7 %psum.52 = f32[]{:T(128)} all-reduce(f32[]{:T(128)} %multiply_reduce_fusion.3), channel_id=1, replica_groups=mesh['mem'=8,'lat'=16] {'lat'}, use_global_device_ids=true, to_apply=%region_8.9 | all-reduce | flops 1 | bytes 8 | tf_op jit(solution)/shard_map/psum | solution.py:94
  359.1 4.5 fusion.3
  363.6 7.5 %fusion.28 = f32[32,24,320]{2,1,0:T(8,128)S(1)} fusion(f32[32,24,1280]{2,1,0:T(8,128)S(1)} %fusion.3, f32[320]{0:T(512)S(1)} %iota_multiply_fusion, f32[1280]{0:T(1024)S(1)} %iota_add_fusion), kind=kOutput, calls=%fused_computation.34 | convolution fusion | flops 3780198400 | bytes 4921600 | tf_op jit(solution)/shard_map/mif,cf->mic/dot_general | solution.py:85
  371.1 1.3 collective-permute-start.13
  372.4 4.6 collective-permute-start.12
  377.0 1.3 collective-permute-done.13
  378.3 1.7 collective-permute-done.12
  380.0 1.3 fusion.36
  381.4 1.3 collective-permute-start.15
  382.7 5.0 collective-permute-start.14
  387.8 5.5 collective-permute-done.15
  393.3 1.7 collective-permute-done.14
  395.0 1.4 multiply_reduce_fusion
  396.5 1.3 collective-permute-start.17
  397.8 5.0 collective-permute-start.16
  402.8 4.3 collective-permute-done.17
  407.2 1.5 collective-permute-done.16
  409.4 1.4 collective-permute-start.19
  410.8 5.3 collective-permute-start.18
  416.1 1.5 collective-permute-done.18
  417.6 1.1 convolution_bitcast_fusion
  418.7 7.7 %fusion.26 = f32[32,24,1280]{2,1,0:T(8,128)S(1)} fusion(f32[32,24,320]{2,1,0:T(8,128)S(1)} %convolution_bitcast_fusion, f32[320]{0:T(512)S(1)} %iota_multiply_fusion, f32[1280]{0:T(1024)S(1)} %iota_add_fusion), kind=kOutput, calls=%fused_computation.33 | convolution fusion | flops 3780198400 | bytes 4921600 | tf_op jit(solution)/shard_map/dot_general | solution.py:70
  426.5 1.9 fusion.4
  428.4 63.4 %all-reduce.8.cloned.1.call-done = f32[3,24,1280]{2,1,0:T(8,128)} async-done(((f32[3,24,1280]{2,1,0:T(8,128)}), f32[3,24,1280]{2,1,0:T(8,128)}) %all-reduce.8.cloned.1.call-update) | async-done | bytes 368656 | tf_op jit(solution)/shard_map/psum | solution.py:77
  491.8 1.7 multiply_reduce_fusion.2
  493.5 64.9 %psum.53 = f32[]{:T(128)} all-reduce(f32[]{:T(128)} %get-tuple-element.28), channel_id=1, replica_groups=mesh['mem'=8,'lat'=16] {'mem','lat'}, use_global_device_ids=true, to_apply=%region_11.12 | all-reduce | flops 1 | bytes 8 | tf_op jit(solution)/shard_map/psum | solution.py:92
  558.4 38.5 %psum.55 = f32[]{:T(128)} all-reduce(f32[]{:T(128)} %multiply_reduce_fusion.2), channel_id=1, replica_groups=mesh['mem'=8,'lat'=16] {'lat'}, use_global_device_ids=true, to_apply=%region_15.16 | all-reduce | flops 1 | bytes 8 | tf_op jit(solution)/shard_map/psum | solution.py:94
  599.8 1.6 dynamic-slice_subtract_fusion
  (57 shorter events, 7.4 us)
Async XLA Ops:
  7.2 103.6 %all-reduce.4.cloned.1.call-start = ((), (), s32[]{:S(2)}) async-start(), calls=%async_computation | async-start | bytes 737280 | tf_op jit(solution)/shard_map/psum | solution.py:77
  8.4 12.6 %collective-permute-start.1 = (f32[32,5,320]{2,1,0:T(8,128)S(1)}, f32[32,5,320]{2,1,0:T(8,128)S(1)}, u32[]{:S(2)}, u32[]{:S(2)}) collective-permute-start(f32[32,5,320]{2,1,0:T(8,128)S(1)} %get-tuple-element.25), channel_id=1, source_target_pairs={{1,0},{2,1},{3,2},{4,3},{5,4},{6,5},{7,6},{8,7},{9,8},{10,9},{11,1... | collective-permute-start | bytes 614408 | tf_op jit(solution)/shard_map/ppermute | solution.py:21
  9.7 12.5 %collective-permute-start = (f32[32,5,320]{2,1,0:T(8,128)S(1)}, f32[32,5,320]{2,1,0:T(8,128)S(1)}, u32[]{:S(2)}, u32[]{:S(2)}) collective-permute-start(f32[32,5,320]{2,1,0:T(8,128)S(1)} %get-tuple-element.24), channel_id=1, source_target_pairs={{0,1},{1,2},{2,3},{3,4},{4,5},{5,6},{6,7},{7,8},{8,9},{9,10},{10,1... | collective-permute-start | bytes 614408 | tf_op jit(solution)/shard_map/ppermute | solution.py:19
  22.2 17.8 %slice-start = ((s8[5898240]{0:T(1024)(128)(4,1)}), s8[4194304]{0:T(1024)(128)(4,1)S(1)}, s32[]{:S(2)}) async-start(s8[5898240]{0:T(1024)(128)(4,1)} %bitcast.63), calls=%async_computation.3 | async-start | bytes 8388608
  23.0 6.6 %collective-permute-start.3 = (f32[32,1,320]{2,1,0:T(1,128)S(1)}, f32[32,1,320]{2,1,0:T(1,128)S(1)}, u32[]{:S(2)}, u32[]{:S(2)}) collective-permute-start(f32[32,1,320]{2,1,0:T(1,128)S(1)} %get-tuple-element.23), channel_id=1, source_target_pairs={{1,0},{2,1},{3,2},{4,3},{5,4},{6,5},{7,6},{8,7},{9,8},{10,9},{11,1... | collective-permute-start | bytes 122888 | tf_op jit(solution)/shard_map/ppermute | solution.py:21
  24.4 6.8 %collective-permute-start.2 = (f32[32,1,320]{2,1,0:T(1,128)S(1)}, f32[32,1,320]{2,1,0:T(1,128)S(1)}, u32[]{:S(2)}, u32[]{:S(2)}) collective-permute-start(f32[32,1,320]{2,1,0:T(1,128)S(1)} %get-tuple-element.22), channel_id=1, source_target_pairs={{0,1},{1,2},{2,3},{3,4},{4,5},{5,6},{6,7},{7,8},{8,9},{9,10},{10,1... | collective-permute-start | bytes 122888 | tf_op jit(solution)/shard_map/ppermute | solution.py:19
  32.3 7.7 %slice-start.1 = ((s8[5898240]{0:T(1024)(128)(4,1)}), s8[1703936]{0:T(1024)(128)(4,1)S(1)}, s32[]{:S(2)}) async-start(s8[5898240]{0:T(1024)(128)(4,1)} %bitcast.63), calls=%async_computation.4 | async-start | bytes 3407872
  40.1 2.5 copy-start.3
  40.1 70.7 %copy-start.1 = (f32[3,24,1280]{2,1,0:T(8,128)S(1)}, f32[3,24,1280]{2,1,0:T(8,128)}, u32[]{:S(2)}) copy-start(f32[3,24,1280]{2,1,0:T(8,128)} %param.6) | copy-start | bytes 1105924
  42.0 208.7 %all-reduce.6.cloned.1.call-start = ((), (), s32[]{:S(2)}) async-start(), calls=%async_computation.1 | async-start | bytes 737280 | tf_op jit(solution)/shard_map/psum | solution.py:77
  123.8 6.5 %collective-permute-start.5 = (f32[32,2,320]{2,1,0:T(2,128)S(1)}, f32[32,2,320]{2,1,0:T(2,128)S(1)}, u32[]{:S(2)}, u32[]{:S(2)}) collective-permute-start(f32[32,2,320]{2,1,0:T(2,128)S(1)} %get-tuple-element.9), channel_id=1, source_target_pairs={{1,0},{2,1},{3,2},{4,3},{5,4},{6,5},{7,6},{8,7},{9,8},{10,9},{11,1... | collective-permute-start | bytes 245768 | tf_op jit(solution)/shard_map/ppermute | solution.py:21
  125.1 6.8 %collective-permute-start.4 = (f32[32,2,320]{2,1,0:T(2,128)S(1)}, f32[32,2,320]{2,1,0:T(2,128)S(1)}, u32[]{:S(2)}, u32[]{:S(2)}) collective-permute-start(f32[32,2,320]{2,1,0:T(2,128)S(1)} %get-tuple-element.8), channel_id=1, source_target_pairs={{0,1},{1,2},{2,3},{3,4},{4,5},{5,6},{6,7},{7,8},{8,9},{9,10},{10,1... | collective-permute-start | bytes 245768 | tf_op jit(solution)/shard_map/ppermute | solution.py:19
  129.7 15.1 %copy-start = (f32[32,6,320]{2,0,1:T(8,128)S(1)}, f32[32,6,320]{2,0,1:T(8,128)}, u32[]{:S(2)}) copy-start(f32[32,6,320]{2,0,1:T(8,128)} %param.5) | copy-start | bytes 737284
  133.3 10.1 %collective-permute-start.7 = (f32[32,5,320]{2,1,0:T(8,128)S(1)}, f32[32,5,320]{2,1,0:T(8,128)S(1)}, u32[]{:S(2)}, u32[]{:S(2)}) collective-permute-start(f32[32,5,320]{2,1,0:T(8,128)S(1)} %get-tuple-element.21), channel_id=1, source_target_pairs={{1,0},{2,1},{3,2},{4,3},{5,4},{6,5},{7,6},{8,7},{9,8},{10,9},{11,1... | collective-permute-start | bytes 614408 | tf_op jit(solution)/shard_map/ppermute | solution.py:21
  134.6 10.2 %collective-permute-start.6 = (f32[32,5,320]{2,1,0:T(8,128)S(1)}, f32[32,5,320]{2,1,0:T(8,128)S(1)}, u32[]{:S(2)}, u32[]{:S(2)}) collective-permute-start(f32[32,5,320]{2,1,0:T(8,128)S(1)} %get-tuple-element.20), channel_id=1, source_target_pairs={{0,1},{1,2},{2,3},{3,4},{4,5},{5,6},{6,7},{7,8},{8,9},{9,10},{10,1... | collective-permute-start | bytes 614408 | tf_op jit(solution)/shard_map/ppermute | solution.py:19
  146.3 10.1 %collective-permute-start.9 = (f32[32,5,320]{2,1,0:T(8,128)S(1)}, f32[32,5,320]{2,1,0:T(8,128)S(1)}, u32[]{:S(2)}, u32[]{:S(2)}) collective-permute-start(f32[32,5,320]{2,1,0:T(8,128)S(1)} %get-tuple-element.19), channel_id=1, source_target_pairs={{1,0},{2,1},{3,2},{4,3},{5,4},{6,5},{7,6},{8,7},{9,8},{10,9},{11,1... | collective-permute-start | bytes 614408 | tf_op jit(solution)/shard_map/ppermute | solution.py:21
  147.6 10.3 %collective-permute-start.8 = (f32[32,5,320]{2,1,0:T(8,128)S(1)}, f32[32,5,320]{2,1,0:T(8,128)S(1)}, u32[]{:S(2)}, u32[]{:S(2)}) collective-permute-start(f32[32,5,320]{2,1,0:T(8,128)S(1)} %get-tuple-element.18), channel_id=1, source_target_pairs={{0,1},{1,2},{2,3},{3,4},{4,5},{5,6},{6,7},{7,8},{8,9},{9,10},{10,1... | collective-permute-start | bytes 614408 | tf_op jit(solution)/shard_map/ppermute | solution.py:19
  157.9 17.8 %slice-start.2 = ((s8[5898240]{0:T(1024)(128)(4,1)}), s8[4194304]{0:T(1024)(128)(4,1)S(1)}, s32[]{:S(2)}) async-start(s8[5898240]{0:T(1024)(128)(4,1)} %bitcast.65), calls=%async_computation.5 | async-start | bytes 8388608
  158.7 6.6 %collective-permute-start.11 = (f32[32,1,320]{2,1,0:T(1,128)S(1)}, f32[32,1,320]{2,1,0:T(1,128)S(1)}, u32[]{:S(2)}, u32[]{:S(2)}) collective-permute-start(f32[32,1,320]{2,1,0:T(1,128)S(1)} %get-tuple-element.17), channel_id=1, source_target_pairs={{1,0},{2,1},{3,2},{4,3},{5,4},{6,5},{7,6},{8,7},{9,8},{10,9},{11,1... | collective-permute-start | bytes 122888 | tf_op jit(solution)/shard_map/ppermute | solution.py:21
  160.1 6.8 %collective-permute-start.10 = (f32[32,1,320]{2,1,0:T(1,128)S(1)}, f32[32,1,320]{2,1,0:T(1,128)S(1)}, u32[]{:S(2)}, u32[]{:S(2)}) collective-permute-start(f32[32,1,320]{2,1,0:T(1,128)S(1)} %get-tuple-element.16), channel_id=1, source_target_pairs={{0,1},{1,2},{2,3},{3,4},{4,5},{5,6},{6,7},{7,8},{8,9},{9,10},{10,1... | collective-permute-start | bytes 122888 | tf_op jit(solution)/shard_map/ppermute | solution.py:19
  168.0 7.7 %slice-start.3 = ((s8[5898240]{0:T(1024)(128)(4,1)}), s8[1703936]{0:T(1024)(128)(4,1)S(1)}, s32[]{:S(2)}) async-start(s8[5898240]{0:T(1024)(128)(4,1)} %bitcast.65), calls=%async_computation.6 | async-start | bytes 3407872
  175.7 182.2 %copy-start.2 = (f32[3,24,1280]{2,1,0:T(8,128)S(1)}, f32[3,24,1280]{2,1,0:T(8,128)}, u32[]{:S(2)}) copy-start(f32[3,24,1280]{2,1,0:T(8,128)} %all-reduce.4.cloned.1.call-done) | copy-start | bytes 1105924
  177.7 314.1 %all-reduce.8.cloned.1.call-start = ((), (), s32[]{:S(2)}) async-start(), calls=%async_computation.2 | async-start | bytes 737280 | tf_op jit(solution)/shard_map/psum | solution.py:77
  371.1 7.2 %collective-permute-start.13 = (f32[32,2,320]{2,1,0:T(2,128)S(1)}, f32[32,2,320]{2,1,0:T(2,128)S(1)}, u32[]{:S(2)}, u32[]{:S(2)}) collective-permute-start(f32[32,2,320]{2,1,0:T(2,128)S(1)} %get-tuple-element.7), channel_id=1, source_target_pairs={{1,0},{2,1},{3,2},{4,3},{5,4},{6,5},{7,6},{8,7},{9,8},{10,9},{11,1... | collective-permute-start | bytes 245768 | tf_op jit(solution)/shard_map/ppermute | solution.py:21
  372.4 7.6 %collective-permute-start.12 = (f32[32,2,320]{2,1,0:T(2,128)S(1)}, f32[32,2,320]{2,1,0:T(2,128)S(1)}, u32[]{:S(2)}, u32[]{:S(2)}) collective-permute-start(f32[32,2,320]{2,1,0:T(2,128)S(1)} %get-tuple-element.6), channel_id=1, source_target_pairs={{0,1},{1,2},{2,3},{3,4},{4,5},{5,6},{6,7},{7,8},{8,9},{9,10},{10,1... | collective-permute-start | bytes 245768 | tf_op jit(solution)/shard_map/ppermute | solution.py:19
  381.4 11.9 %collective-permute-start.15 = (f32[32,5,320]{2,1,0:T(8,128)S(1)}, f32[32,5,320]{2,1,0:T(8,128)S(1)}, u32[]{:S(2)}, u32[]{:S(2)}) collective-permute-start(f32[32,5,320]{2,1,0:T(8,128)S(1)} %get-tuple-element.15), channel_id=1, source_target_pairs={{1,0},{2,1},{3,2},{4,3},{5,4},{6,5},{7,6},{8,7},{9,8},{10,9},{11,1... | collective-permute-start | bytes 614408 | tf_op jit(solution)/shard_map/ppermute | solution.py:21
  382.7 12.3 %collective-permute-start.14 = (f32[32,5,320]{2,1,0:T(8,128)S(1)}, f32[32,5,320]{2,1,0:T(8,128)S(1)}, u32[]{:S(2)}, u32[]{:S(2)}) collective-permute-start(f32[32,5,320]{2,1,0:T(8,128)S(1)} %get-tuple-element.14), channel_id=1, source_target_pairs={{0,1},{1,2},{2,3},{3,4},{4,5},{5,6},{6,7},{7,8},{8,9},{9,10},{10,1... | collective-permute-start | bytes 614408 | tf_op jit(solution)/shard_map/ppermute | solution.py:19
  396.5 10.7 %collective-permute-start.17 = (f32[32,5,320]{2,1,0:T(8,128)S(1)}, f32[32,5,320]{2,1,0:T(8,128)S(1)}, u32[]{:S(2)}, u32[]{:S(2)}) collective-permute-start(f32[32,5,320]{2,1,0:T(8,128)S(1)} %get-tuple-element.13), channel_id=1, source_target_pairs={{1,0},{2,1},{3,2},{4,3},{5,4},{6,5},{7,6},{8,7},{9,8},{10,9},{11,1... | collective-permute-start | bytes 614408 | tf_op jit(solution)/shard_map/ppermute | solution.py:21
  397.8 10.8 %collective-permute-start.16 = (f32[32,5,320]{2,1,0:T(8,128)S(1)}, f32[32,5,320]{2,1,0:T(8,128)S(1)}, u32[]{:S(2)}, u32[]{:S(2)}) collective-permute-start(f32[32,5,320]{2,1,0:T(8,128)S(1)} %get-tuple-element.12), channel_id=1, source_target_pairs={{0,1},{1,2},{2,3},{3,4},{4,5},{5,6},{6,7},{7,8},{8,9},{9,10},{10,1... | collective-permute-start | bytes 614408 | tf_op jit(solution)/shard_map/ppermute | solution.py:19
  408.6 17.8 %slice-start.4 = ((s8[5898240]{0:T(1024)(128)(4,1)}), s8[4194304]{0:T(1024)(128)(4,1)S(1)}, s32[]{:S(2)}) async-start(s8[5898240]{0:T(1024)(128)(4,1)} %bitcast.67), calls=%async_computation.7 | async-start | bytes 8388608
  409.4 6.7 %collective-permute-start.19 = (f32[32,1,320]{2,1,0:T(1,128)S(1)}, f32[32,1,320]{2,1,0:T(1,128)S(1)}, u32[]{:S(2)}, u32[]{:S(2)}) collective-permute-start(f32[32,1,320]{2,1,0:T(1,128)S(1)} %get-tuple-element.11), channel_id=1, source_target_pairs={{1,0},{2,1},{3,2},{4,3},{5,4},{6,5},{7,6},{8,7},{9,8},{10,9},{11,1... | collective-permute-start | bytes 122888 | tf_op jit(solution)/shard_map/ppermute | solution.py:21
  410.8 6.8 %collective-permute-start.18 = (f32[32,1,320]{2,1,0:T(1,128)S(1)}, f32[32,1,320]{2,1,0:T(1,128)S(1)}, u32[]{:S(2)}, u32[]{:S(2)}) collective-permute-start(f32[32,1,320]{2,1,0:T(1,128)S(1)} %get-tuple-element.10), channel_id=1, source_target_pairs={{0,1},{1,2},{2,3},{3,4},{4,5},{5,6},{6,7},{7,8},{8,9},{9,10},{10,1... | collective-permute-start | bytes 122888 | tf_op jit(solution)/shard_map/ppermute | solution.py:19
  418.7 7.7 %slice-start.5 = ((s8[5898240]{0:T(1024)(128)(4,1)}), s8[1703936]{0:T(1024)(128)(4,1)S(1)}, s32[]{:S(2)}) async-start(s8[5898240]{0:T(1024)(128)(4,1)} %bitcast.67), calls=%async_computation.8 | async-start | bytes 3407872
Sparse Core Ops, SparseCore 0:
  42.2 68.5 all-reduce.3
  177.8 72.8 all-reduce.5
  428.5 63.2 all-reduce.7
where the time goes:
time: 618 us; the launch traced here: 608 us
  waiting for transfers between devices  246 us (40%)
  blocking collectives  207 us (33%)
  starting transfers between devices  63.1 us (10%)
  matrix products  48.9 us (8%)
  other arithmetic  22.3 us (4%)
  between operations  18.6 us (3%)
    psum x3, waiting for transfers between devices, combine_members(): return lax.psum(partial_value, 'mem')  205 us
    psum x2, blocking collectives, per_device(): grad_sq = lax.psum(jnp.sum(gradient * gradient), ('mem', 'lat'))  130 us
    psum x2, blocking collectives, per_device(): image_sq = lax.psum(jnp.sum(image * image), 'lat')  77.1 us
    ppermute x10, starting transfers between devices, with_halo(): lax.ppermute(tail, axis, [(i, (i + 1) % count) for i in range(ends)])  49.2 us
    ppermute x10, waiting for transfers between devices, with_halo(): lax.ppermute(head, axis, [((i + 1) % count, i) for i in range(ends)])  26.2 us
    dot_general x3, matrix products, forward(): jnp.dot(rowwise.reshape(members * fine_rows, coarse_cols), lon_up, precis...  23.1 us
    ppermute x10, waiting for transfers between devices, with_halo(): lax.ppermute(tail, axis, [(i, (i + 1) % count) for i in range(ends)])  15.2 us
    dot_general x2, matrix products, per_device(): columns = jnp.einsum('mif,cf->mic', weighted, lon_up, precision=highest)  14.9 us
  transfers between devices with their start and end apart: 23, of which 21 were waited for; matrix products, arithmetic and copies ran while one was open for 0% of the time, Pallas kernels for 0%

commit v1 on v0

v1 whole, which is shorter than its diff:
```python
import functools

import jax
import jax.numpy as jnp
import numpy as np
from jax import lax
from jax.experimental import pallas as pl
from jax.experimental.pallas import tpu as pltpu
from jax.sharding import PartitionSpec as P

RATIO = 4
HALF = 5
STEPS = 2
GROUP = 8
LANES = 128
MESH = pl.DeviceIdType.MESH
SCALE = 96.0


def tent(distance):
    return np.maximum(0.0, 1.0 - np.abs(distance) / RATIO)


def row_operator(coarse_rows, first, last):
    fine = np.arange(RATIO * coarse_rows)[:, None]
    inner = np.arange(-1, coarse_rows + 1)
    up = tent(fine + 0.5 - RATIO * inner[None, :] - RATIO / 2)
    if first:
        up[:, 0] = 0.0
    if last:
        up[:, -1] = 0.0
    outer = np.arange(-coarse_rows, 2 * coarse_rows)
    gap = np.abs(inner[:, None] - outer[None, :])
    smooth = np.where(gap <= HALF, (1.0 - gap / (HALF + 1)) / 2, 0.0)
    return np.rint(SCALE * up @ smooth)


def block_rows(operator):
    fine, wide = operator.shape
    out = np.zeros((GROUP, fine, wide, GROUP))
    for member in range(GROUP):
        out[member, :, :, member] = operator
    return out.reshape(GROUP * fine, wide * GROUP)


def tables(coarse_rows):
    ops = [block_rows(row_operator(coarse_rows, *ends)) for ends in ((True, False), (False, False), (False, True))]
    rows_up = np.stack(ops)
    rows_down = np.stack([op.T for op in ops])
    fine = np.arange(2 * LANES)[None, :]
    narrow = tent(LANES + fine + 0.5 - RATIO * np.arange(LANES)[:, None] - RATIO / 2)
    wide = tent(3 * LANES + fine + 0.5 - RATIO * np.arange(2 * LANES)[:, None] - RATIO / 2)
    narrow_up = np.concatenate([narrow, narrow], 0)
    narrow_down = np.concatenate([narrow.T, narrow.T], 0)
    wide_down = np.concatenate([wide.T, wide.T], 0)
    return [jnp.asarray(t, jnp.bfloat16) for t in (rows_up, rows_down, narrow_up, wide, narrow_down, wide_down)]


def split(x):
    high = x.astype(jnp.bfloat16)
    return high, (x - high.astype(jnp.float32)).astype(jnp.bfloat16)


def dot(a, b):
    return jnp.dot(a, b, preferred_element_type=jnp.float32)


def kernel(
    n_mem, n_lat, seg,
    pert_hbm, control, innov, thr, rows_up, rows_down, narrow_up, wide_up, narrow_down, wide_down,
    weights_out, inc_out,
    pert, halo, part_send, part_recv, own, w, acc, gather, inc, misfit, obs, rs_recv,
    sc_lat_send, sc_lat, sc_mem_send, sc_mem,
    pert_sem, g_send, g_recv, c_send, c_recv, rs_ss, rs_rs, ag_ss, ag_rs, sl_ss, sl_rs, sm_ss, sm_rs,
):
    mem = lax.axis_index("mem")
    lat = lax.axis_index("lat")
    chunks = pert.shape[0] // GROUP
    n_vars = pert.shape[1]
    fine = pert.shape[2]
    tiles = pert.shape[3] // LANES
    tile_rows = n_vars * fine
    part = gather.shape[0] // n_mem
    half = seg // 2
    case = jnp.where(lat == 0, 0, jnp.where(lat == n_lat - 1, 2, 1))
    up_id = (mem, jnp.maximum(lat - 1, 0))
    down_id = (mem, jnp.minimum(lat + 1, n_lat - 1))
    has_up = lat > 0
    has_down = lat < n_lat - 1

    def pert_copy(c):
        rows = pl.ds(c * GROUP, GROUP)
        return pltpu.make_async_copy(pert_hbm.at[rows], pert.at[rows], pert_sem.at[c])

    for c in range(chunks):
        pert_copy(c).start()

    barrier = pltpu.get_barrier_semaphore()
    for k in range(1, n_mem):
        pl.semaphore_signal(barrier, inc=1, device_id=(lax.rem(mem + k, n_mem), lat), device_id_type=MESH)
    for k in range(1, n_lat):
        pl.semaphore_signal(barrier, inc=1, device_id=(mem, lax.rem(lat + k, n_lat)), device_id_type=MESH)
    pl.semaphore_wait(barrier, n_mem + n_lat - 2)

    def g_copy(c, up):
        return pltpu.make_async_remote_copy(
            src_ref=halo.at[1, c], dst_ref=halo.at[2 if up else 0, c],
            send_sem=g_send.at[0 if up else 1, c], recv_sem=g_recv.at[0 if up else 1, c],
            device_id=up_id if up else down_id, device_id_type=MESH)

    def c_copy(c, up):
        return pltpu.make_async_remote_copy(
            src_ref=part_send.at[0 if up else 1, c], dst_ref=part_recv.at[0 if up else 1, c],
            send_sem=c_send.at[0 if up else 1, c], recv_sem=c_recv.at[0 if up else 1, c],
            device_id=up_id if up else down_id, device_id_type=MESH)

    def send_both(copy, c):
        @pl.when(has_up)
        def _():
            copy(c, True).start()

        @pl.when(has_down)
        def _():
            copy(c, False).start()

    def recv_both(copy, c):
        @pl.when(has_down)
        def _():
            copy(c, True).wait_recv()

        @pl.when(has_up)
        def _():
            copy(c, False).wait_recv()

    def sent_both(copy, c):
        @pl.when(has_up)
        def _():
            copy(c, True).wait_send()

        @pl.when(has_down)
        def _():
            copy(c, False).wait_send()

    lane = lax.broadcasted_iota(jnp.int32, (half, LANES), 1)
    left = lane < LANES // 2

    def swap(x):
        return pltpu.roll(x, LANES // 2, 1)

    def pack(x, factor):
        e0, e1, e2 = x[:, :LANES], x[:, LANES:2 * LANES], x[:, 2 * LANES:]
        a, b = e2[:half], e2[half:]
        sa, sb = swap(a), swap(b)
        top = e0[:half] + jnp.where(left, sa, 0.0)
        bottom = e0[half:] + jnp.where(left, sb, 0.0)
        tail = jnp.where(left, a, sb)
        return jnp.concatenate([top, bottom, e1, tail], axis=0) * factor

    def unpack(x):
        e0, e1, tail = x[:seg], x[seg:2 * seg], x[2 * seg:]
        st = swap(tail)
        a = jnp.where(left, tail, swap(e0[:half]))
        b = jnp.where(left, st, swap(e0[half:]))
        return jnp.concatenate([e0, e1, jnp.concatenate([a, b], axis=0)], axis=1)

    def lane_pair(j):
        return 2 * j + 1, (2 * j + 2) % tiles

    def forward_chunk(c):
        block = jnp.concatenate([unpack(halo[s, c]) for s in range(3)], axis=0)
        high, low = split(block)
        table = rows_up[case]
        rows = dot(table, high) + dot(table, low)
        high, low = split(rows)
        members = pl.ds(c * GROUP, GROUP)
        for j in range(tiles // 2):
            g = j // 2
            cols = slice(g * LANES, (g + 1) * LANES)
            if j % 2 == 0:
                fine_rows = dot(jnp.concatenate([high[:, cols], low[:, cols]], axis=1), narrow_up[...])
            else:
                cols = slice(g * LANES, (g + 2) * LANES)
                fine_rows = dot(high[:, cols], wide_up[...]) + dot(low[:, cols], wide_up[...])
            for h, t in enumerate(lane_pair(j)):
                field = fine_rows[:, h * LANES:(h + 1) * LANES].reshape(GROUP, fine, LANES)
                for v in range(n_vars):
                    p = pert[members, v, :, t * LANES:(t + 1) * LANES].astype(jnp.float32)
                    where = pl.ds(t * tile_rows + v * fine, fine)
                    acc[where, :] += jnp.sum(p * field, axis=0)

    def adjoint_chunk(c):
        members = pl.ds(c * GROUP, GROUP)
        sums = [None] * 3

        def add(i, value):
            sums[i] = value if sums[i] is None else sums[i] + value

        for j in range(tiles // 2):
            pieces = []
            for t in lane_pair(j):
                total = None
                for v in range(n_vars):
                    p = pert[members, v, :, t * LANES:(t + 1) * LANES].astype(jnp.float32)
                    term = p * misfit[pl.ds(t * tile_rows + v * fine, fine), :][None]
                    total = term if total is None else total + term
                pieces.append(split(total.reshape(GROUP * fine, LANES)))
            lhs = jnp.concatenate([pieces[0][0], pieces[1][0], pieces[0][1], pieces[1][1]], axis=1)
            g = j // 2
            if j % 2 == 0:
                add(g, dot(lhs, narrow_down[...]))
            else:
                both = dot(lhs, wide_down[...])
                add(g, both[:, :LANES])
                add(g + 1, both[:, LANES:])
        high, low = split(jnp.concatenate(sums, axis=1))
        table = rows_down[case]
        coarse = dot(table, high) + dot(table, low)
        part_send[0, c] = pack(coarse[:seg], 1.0 / SCALE)
        own[c] = pack(coarse[seg:2 * seg], 1.0 / SCALE)
        part_send[1, c] = pack(coarse[2 * seg:], 1.0 / SCALE)

    def forward_all():
        acc[...] = jnp.zeros_like(acc)

        def body(c, carry):
            recv_both(g_copy, c)
            forward_chunk(c)
            return carry

        lax.fori_loop(0, chunks, body, 0)

        def body_sent(c, carry):
            sent_both(g_copy, c)
            return carry

        lax.fori_loop(0, chunks, body_sent, 0)

    def part_rows(k):
        return pl.ds(pl.multiple_of(k * part, 8), part)

    def rs_copy(k):
        peer = lax.rem(mem + k, n_mem)
        return pltpu.make_async_remote_copy(
            src_ref=acc.at[part_rows(peer)], dst_ref=rs_recv.at[k - 1],
            send_sem=rs_ss.at[k - 1], recv_sem=rs_rs.at[k - 1], device_id=(peer, lat), device_id_type=MESH)

    def ag_copy(k):
        peer = lax.rem(mem + k, n_mem)
        return pltpu.make_async_remote_copy(
            src_ref=gather.at[part_rows(mem)], dst_ref=gather.at[part_rows(mem)],
            send_sem=ag_ss.at[k - 1], recv_sem=ag_rs.at[k - 1], device_id=(peer, lat), device_id_type=MESH)

    def reduce_scatter():
        for k in range(1, n_mem):
            rs_copy(k).start()
        for k in range(1, n_mem):
            rs_copy(k).wait_recv()
        total = acc[part_rows(mem), :]
        for k in range(1, n_mem):
            total = total + rs_recv[k - 1]
        total = total * (1.0 / SCALE)
        gather[part_rows(mem), :] = total
        for k in range(1, n_mem):
            rs_copy(k).wait_send()
        return total

    def gather_start():
        for k in range(1, n_mem):
            ag_copy(k).start()

    def gather_wait():
        for k in range(1, n_mem):
            ag_copy(k).wait_recv()
        for k in range(1, n_mem):
            ag_copy(k).wait_send()

    def sl_copy(it, k):
        return pltpu.make_async_remote_copy(
            src_ref=sc_lat_send, dst_ref=sc_lat.at[it, k - 1],
            send_sem=sl_ss.at[it, k - 1], recv_sem=sl_rs.at[it, k - 1],
            device_id=(mem, lax.rem(lat + k, n_lat)), device_id_type=MESH)

    def sm_copy(it, k):
        return pltpu.make_async_remote_copy(
            src_ref=sc_mem_send, dst_ref=sc_mem.at[it, k - 1],
            send_sem=sm_ss.at[it, k - 1], recv_sem=sm_rs.at[it, k - 1],
            device_id=(lax.rem(mem + k, n_mem), lat), device_id_type=MESH)

    def total_of(squares):
        return jnp.sum(squares.reshape(-1, 8, LANES), axis=0)

    zero = jnp.zeros(halo.shape[2:], jnp.float32)

    def start_body(c, carry):
        halo[1, c] = control[c]
        w[c] = control[c]
        send_both(g_copy, c)
        return carry

    lax.fori_loop(0, chunks, start_body, 0)

    @pl.when(jnp.logical_not(has_up))
    def _():
        for c in range(chunks):
            halo[0, c] = zero
            part_recv[1, c] = zero

    @pl.when(jnp.logical_not(has_down))
    def _():
        for c in range(chunks):
            halo[2, c] = zero
            part_recv[0, c] = zero

    for t in range(tiles):
        for v in range(n_vars):
            obs[pl.ds(t * tile_rows + v * fine, fine), :] = innov[v, :, t * LANES:(t + 1) * LANES]

    for c in range(chunks):
        pert_copy(c).wait()
    forward_all()
    reduce_scatter()
    gather_start()
    gather_wait()
    inc[...] = gather[: tiles * tile_rows, :]

    def step(it, carry):
        for t in range(tiles):
            for v in range(n_vars):
                rows = pl.ds(t * tile_rows + v * fine, fine)
                misfit[rows, :] = jnp.clip(inc[rows, :] - obs[rows, :], -thr[v], thr[v])

        def adjoint_body(c, carry):
            adjoint_chunk(c)
            send_both(c_copy, c)
            return carry

        lax.fori_loop(0, chunks, adjoint_body, 0)

        def gradient_body(c, squares):
            recv_both(c_copy, c)
            grad = w[c] + own[c] + part_recv[0, c] + part_recv[1, c]
            halo[1, c] = grad
            send_both(g_copy, c)
            sent_both(c_copy, c)
            return squares + total_of(grad * grad)

        grad_sq = lax.fori_loop(0, chunks, gradient_body, jnp.zeros((8, LANES), jnp.float32))
        forward_all()
        piece = reduce_scatter()
        gather_start()
        image_sq = total_of(piece * piece)
        row = lax.broadcasted_iota(jnp.int32, (8, LANES), 0)
        sums = jnp.where(
            row == 0, jnp.sum(grad_sq, axis=0, keepdims=True),
            jnp.where(row == 1, jnp.sum(image_sq, axis=0, keepdims=True), 0.0))
        sc_lat_send[...] = sums
        for k in range(1, n_lat):
            sl_copy(it, k).start()
        for k in range(1, n_lat):
            sl_copy(it, k).wait_recv()
        for k in range(1, n_lat):
            sums = sums + sc_lat[it, k - 1]
        sc_mem_send[...] = sums
        for k in range(1, n_mem):
            sm_copy(it, k).start()
        for k in range(1, n_mem):
            sm_copy(it, k).wait_recv()
        for k in range(1, n_mem):
            sums = sums + sc_mem[it, k - 1]
        g2 = jnp.sum(sums[0:1, :], axis=1, keepdims=True)
        h2 = jnp.sum(sums[1:2, :], axis=1, keepdims=True)
        step_len = g2 / (g2 + h2)
        for c in range(chunks):
            w[c] = w[c] - step_len * halo[1, c]
        gather_wait()
        inc[...] = inc[...] - step_len * gather[: tiles * tile_rows, :]
        for k in range(1, n_lat):
            sl_copy(it, k).wait_send()
        for k in range(1, n_mem):
            sm_copy(it, k).wait_send()
        return carry

    lax.fori_loop(0, STEPS, step, 0)
    weights_out[...] = w[...]
    inc_out[...] = inc[...]


def per_device(n_mem, n_lat, perturbations, control, innovations, thresholds):
    members, coarse_rows, coarse_cols = control.shape
    n_vars, fine_rows, fine_cols = innovations.shape
    chunks = members // GROUP
    seg = GROUP * coarse_rows
    packed = seg * coarse_cols // LANES
    half = seg // 2
    tail = coarse_cols - 2 * LANES
    flat = n_vars * fine_rows * fine_cols // LANES
    part = -(-flat // n_mem // 8) * 8
    ordered = control.reshape(chunks, GROUP, coarse_rows, coarse_cols).transpose(0, 2, 1, 3).reshape(chunks, seg, coarse_cols)
    ends = ordered[:, :, 2 * LANES:]
    ordered = jnp.concatenate(
        [ordered[:, :, :LANES], ordered[:, :, LANES:2 * LANES], jnp.concatenate([ends[:, :half], ends[:, half:]], axis=2)], axis=1)
    vmem = pl.BlockSpec(memory_space=pltpu.VMEM)
    f32 = jnp.float32
    dma = pltpu.SemaphoreType.DMA
    weights, increment = pl.pallas_call(
        functools.partial(kernel, n_mem, n_lat, seg),
        out_shape=(jax.ShapeDtypeStruct((chunks, packed, LANES), f32), jax.ShapeDtypeStruct((flat, LANES), f32)),
        in_specs=[pl.BlockSpec(memory_space=pl.ANY), vmem, vmem, pl.BlockSpec(memory_space=pltpu.SMEM)] + [vmem] * 6,
        out_specs=(vmem, vmem),
        scratch_shapes=[
            pltpu.VMEM(perturbations.shape, jnp.bfloat16),
            pltpu.VMEM((3, chunks, packed, LANES), f32),
            pltpu.VMEM((2, chunks, packed, LANES), f32),
            pltpu.VMEM((2, chunks, packed, LANES), f32),
            pltpu.VMEM((chunks, packed, LANES), f32),
            pltpu.VMEM((chunks, packed, LANES), f32),
            pltpu.VMEM((n_mem * part, LANES), f32),
            pltpu.VMEM((n_mem * part, LANES), f32),
            pltpu.VMEM((flat, LANES), f32),
            pltpu.VMEM((flat, LANES), f32),
            pltpu.VMEM((flat, LANES), f32),
            pltpu.VMEM((n_mem - 1, part, LANES), f32),
            pltpu.VMEM((8, LANES), f32),
            pltpu.VMEM((STEPS, n_lat - 1, 8, LANES), f32),
            pltpu.VMEM((8, LANES), f32),
            pltpu.VMEM((STEPS, n_mem - 1, 8, LANES), f32),
            dma((chunks,)),
            dma((2, chunks)), dma((2, chunks)), dma((2, chunks)), dma((2, chunks)),
            dma((n_mem - 1,)), dma((n_mem - 1,)), dma((n_mem - 1,)), dma((n_mem - 1,)),
            dma((STEPS, n_lat - 1)), dma((STEPS, n_lat - 1)), dma((STEPS, n_mem - 1)), dma((STEPS, n_mem - 1)),
        ],
        compiler_params=pltpu.CompilerParams(collective_id=0, has_side_effects=True),
    )(perturbations, ordered, innovations, thresholds, *tables(coarse_rows))
    ends = weights[:, 2 * seg:]
    ends = jnp.concatenate([ends[:, :, :tail], ends[:, :, tail:]], axis=1)
    weights = jnp.concatenate([weights[:, :seg], weights[:, seg:2 * seg], ends], axis=2)
    weights = weights.reshape(chunks, coarse_rows, GROUP, coarse_cols).transpose(0, 2, 1, 3).reshape(members, coarse_rows, coarse_cols)
    increment = increment.reshape(fine_cols // LANES, n_vars, fine_rows, LANES).transpose(1, 2, 0, 3).reshape(n_vars, fine_rows, fine_cols)
    share = fine_cols // n_mem
    increment = lax.dynamic_slice_in_dim(increment, lax.axis_index("mem") * share, share, 2)
    return weights, increment


def solution(mesh):
    return jax.shard_map(
        functools.partial(per_device, mesh.shape["mem"], mesh.shape["lat"]),
        mesh=mesh,
        in_specs=(P("mem", None, "lat", None), P("mem", "lat", None), P(None, "lat", None), P()),
        out_specs=(P("mem", "lat", None), P(None, "lat", "mem")),
        check_vma=False,
    )
```

time: 618 us -> 99 us (0.16); the launches traced: 608 us -> 97.7 us
  waiting for transfers between devices: 246 us -> 0 us
  blocking collectives: 207 us -> 0 us
  Pallas kernels: 0 us -> 90.7 us
  starting transfers between devices: 63.1 us -> 0 us
  matrix products: 48.9 us -> 0 us
  other arithmetic: 22.3 us -> 1.52 us
  between operations: 18.6 us -> 0.68 us
    psum x4 -> x0, blocking collectives: 207 us -> none  [the longest x2 130 us: per_device(): grad_sq = lax.psum(jnp.sum(gradient * gradient), ('mem', 'lat'))]
    psum x3 -> x0, waiting for transfers between devices: 205 us -> none  [combine_members(): return lax.psum(partial_value, 'mem')]
    pallas_call x0 -> x1, Pallas kernels: none -> 90.7 us  [per_device(): pl.pallas_call(functools.partial(kernel, n_mem, n_lat, seg), out_shape=(j...]
    ppermute x20 -> x0, starting transfers between devices: 62.5 us -> none  [the longest x10 49.2 us: with_halo(): lax.ppermute(tail, axis, [(i, (i + 1) % count) for i in range(ends)])]
    dot_general x15 -> x0, matrix products: 48.9 us -> none  [the longest x3 23.1 us: forward(): jnp.dot(rowwise.reshape(members * fine_rows, coarse_cols), lon_up, precis...]
    ppermute x20 -> x0, waiting for transfers between devices: 41.4 us -> none  [the longest x10 26.2 us: with_halo(): lax.ppermute(head, axis, [((i + 1) % count, i) for i in range(ends)])]
    reduce_sum x7 -> x0, other arithmetic: 18.2 us -> none  [the longest x2 8.98 us: per_device(): weighted = jnp.sum(perturbations.astype(jnp.float32) * misfit[None], axis=1)]
  transfers between devices with their start and end apart: 23 -> 0, of which waited for: 21 -> 0; matrix products, arithmetic and copies ran while one was open for 0% -> 0% of each run, Pallas kernels for 0% -> 0%
where the time goes in v1:
time: 99 us; the launch traced here: 97.7 us
  Pallas kernels  90.7 us (92%)
  local copies, waits for them, and re-layouts  4.79 us (5%)
  other arithmetic  1.52 us (2%)
    pallas_call x1, Pallas kernels, per_device(): pl.pallas_call(functools.partial(kernel, n_mem, n_lat, seg), out_shape=(j...  90.7 us

profile of v1, /device:TPU:0, one launch (start us, length us, event | category | flops | bytes accessed | tf_op | source)
XLA Modules:
  0.0 97.7 jit_solution(7511732300519276522)
XLA Ops:
  0.6 0.0 copy-start
  0.6 1.0 copy-done
  1.7 0.8 maximum_maximum_fusion.control
  2.4 90.7 %shard_map.113 = (f32[4,120,128]{2,1,0:T(8,128)}, f32[720,128]{1,0:T(8,128)}) custom-call(bf16[32,3,24,1280]{3,2,1,0:T(8,128)(2,1)} %pert_hbm.1, f32[4,120,128]{2,1,0:T(8,128)} %maximum_maximum_fusion.control, f32[3,24,1280]{2,1,0:T(8,128)} %innov.1, f32[3]{0:T(128)} %thr.1, bf16[3,192,144]{2,1,0:T(8,128)(2,1)} %constant.24.clone.rows_up, ...), custom_call_target="tpu_custom_call" | custom-call | tf_op jit(solution)/shard_map/pallas_call | solution.py:405
  93.2 1.0 fusion.2
  94.1 1.0 fusion.3
  95.1 0.7 copy_bitcast_fusion.1
  95.8 1.1 %copy.21 = f32[10,3,24,128]{3,0,2,1:T(8,128)S(1)} copy(f32[10,3,24,128]{3,2,1,0:T(8,128)} %bitcast.19) | data formatting | bytes 737280 | tf_op jit(solution)/shard_map/reshape | solution.py:438
  96.9 0.1 reshape.27
  97.0 0.7 constant_dynamic-slice_fusion
  (3 shorter events, 0.0 us)
Async XLA Ops:
  0.6 1.0 copy-start

commit v2 on v0

v2 whole, which is shorter than its diff:
```python
import functools

import jax
import jax.numpy as jnp
import numpy as np
from jax import lax
from jax.experimental import pallas as pl
from jax.experimental.pallas import tpu as pltpu
from jax.sharding import PartitionSpec as P

RATIO = 4
HALF = 5
STEPS = 2
GROUP = 8
PAIR = 2
LANES = 128
MESH = pl.DeviceIdType.MESH
SCALE = 96.0


def tent(distance):
    return np.maximum(0.0, 1.0 - np.abs(distance) / RATIO)


def row_operator(coarse_rows, first, last):
    fine = np.arange(RATIO * coarse_rows)[:, None]
    inner = np.arange(-1, coarse_rows + 1)
    up = tent(fine + 0.5 - RATIO * inner[None, :] - RATIO / 2)
    if first:
        up[:, 0] = 0.0
    if last:
        up[:, -1] = 0.0
    outer = np.arange(-coarse_rows, 2 * coarse_rows)
    gap = np.abs(inner[:, None] - outer[None, :])
    smooth = np.where(gap <= HALF, (1.0 - gap / (HALF + 1)) / 2, 0.0)
    return np.rint(SCALE * up @ smooth)


def block_rows(operator):
    fine, wide = operator.shape
    out = np.zeros((GROUP, fine, wide, GROUP))
    for member in range(GROUP):
        out[member, :, :, member] = operator
    return out.reshape(GROUP * fine, wide * GROUP)


def tables(coarse_rows):
    ops = [block_rows(row_operator(coarse_rows, *ends)) for ends in ((True, False), (False, False), (False, True))]
    rows_up = np.stack(ops)
    rows_down = np.stack([op.T for op in ops])
    fine = np.arange(2 * LANES)[None, :]
    narrow = tent(LANES + fine + 0.5 - RATIO * np.arange(LANES)[:, None] - RATIO / 2)
    wide = tent(3 * LANES + fine + 0.5 - RATIO * np.arange(2 * LANES)[:, None] - RATIO / 2)
    narrow_up = np.concatenate([narrow, narrow], 0)
    wide_up = np.concatenate([wide[:LANES], wide[:LANES], wide[LANES:], wide[LANES:]], 0)
    narrow_down = np.concatenate([narrow.T, narrow.T], 0)
    wide_down = np.concatenate([wide.T, wide.T], 0)
    return [jnp.asarray(t, jnp.bfloat16) for t in (rows_up, rows_down, narrow_up, wide_up, narrow_down, wide_down)]


def split(x):
    high = x.astype(jnp.bfloat16)
    return high, (x - high.astype(jnp.float32)).astype(jnp.bfloat16)


def dot(a, b):
    return jnp.dot(a, b, preferred_element_type=jnp.float32)


def kernel(
    n_mem, n_lat, seg, layout,
    pert_hbm, control_hbm, innov_hbm, thr, rows_up_hbm, rows_down_hbm, narrow_up_hbm, wide_up_hbm, narrow_down_hbm, wide_down_hbm,
    weights_out, inc_out,
    pert_raw, pert, control, innov, rows_up, rows_down, narrow_up, wide_up, narrow_down, wide_down,
    halo, part_send, part_recv, own, w, spare, lifted, acc, pair_recv, half_sum, z_recv, image, inc, misfit, obs,
    lat_send, lat_recv, mem_send, mem_recv,
    pert_sem, load_sem, g_send, g_recv, c_send, c_recv, p_ss, p_rs, z_ss, z_rs, ag_ss, ag_rs, im_ss, im_rs, sl_ss, sl_rs, sm_ss, sm_rs,
):
    mem = lax.axis_index("mem")
    lat = lax.axis_index("lat")
    core = lax.rem(mem, 2)
    n_z = n_mem // 2
    z = mem // 2
    blocks = pert.shape[0] // GROUP
    chunks = blocks // PAIR
    n_vars = pert.shape[1]
    fine = pert.shape[2]
    tiles = pert.shape[3] // LANES
    pairs = tiles // 2
    tile_rows = n_vars * fine
    half = seg // 2
    n_rows = seg // GROUP
    case = jnp.where(lat == 0, 0, jnp.where(lat == n_lat - 1, 2, 1))
    up_id = (mem, jnp.maximum(lat - 1, 0))
    down_id = (mem, jnp.minimum(lat + 1, n_lat - 1))
    has_up = lat > 0
    has_down = lat < n_lat - 1
    partner = (2 * z + 1 - core, lat)
    z_peers = [(2 * lax.rem(z + k, n_z) + core, lat) for k in range(1, n_z)]
    mem_peers = [(lax.rem(mem + k, n_mem), lat) for k in range(1, n_mem)]
    lat_peers = [(mem, lax.rem(lat + k, n_lat)) for k in range(1, n_lat)]
    groups = ((0, seg), (seg, seg + half))
    tail_rows = pl.ds(2 * seg, half)
    bases, parts, starts = layout
    z_bases = [sum(parts[:i]) for i in range(3)]

    loads = [
        (control_hbm, control), (rows_up_hbm.at[case], rows_up), (narrow_up_hbm, narrow_up), (wide_up_hbm, wide_up),
        (innov_hbm, innov), (rows_down_hbm.at[case], rows_down), (narrow_down_hbm, narrow_down), (wide_down_hbm, wide_down),
    ]
    loads = [pltpu.make_async_copy(src, dst, load_sem.at[i]) for i, (src, dst) in enumerate(loads)]

    loads[0].start()
    barrier = pltpu.get_barrier_semaphore()
    for peer in lat_peers + mem_peers:
        pl.semaphore_signal(barrier, inc=1, device_id=peer, device_id_type=MESH)

    def pert_copy(c):
        rows = pl.ds(c * GROUP, GROUP)
        return pltpu.make_async_copy(pert_hbm.at[rows], pert_raw.at[rows], pert_sem.at[c])

    for load in loads[1:4]:
        load.start()
    for c in range(blocks):
        pert_copy(c).start()
    for load in loads[4:]:
        load.start()

    lane = lax.broadcasted_iota(jnp.int32, (half, LANES), 1)
    left = lane < LANES // 2

    def swap(x):
        return pltpu.roll(x, LANES // 2, 1)

    def g_copy(q, b, up):
        rows = pl.ds(*groups[q])
        i = 0 if up else 1
        return pltpu.make_async_remote_copy(
            src_ref=halo.at[1, b, rows], dst_ref=halo.at[2 if up else 0, b, rows],
            send_sem=g_send.at[i, q, b], recv_sem=g_recv.at[i, q, b],
            device_id=up_id if up else down_id, device_id_type=MESH)

    def c_copy(q, b, up):
        rows = pl.ds(*groups[q])
        i = 0 if up else 1
        return pltpu.make_async_remote_copy(
            src_ref=part_send.at[i, b, rows], dst_ref=part_recv.at[i, b, rows],
            send_sem=c_send.at[i, q, b], recv_sem=c_recv.at[i, q, b],
            device_id=up_id if up else down_id, device_id_type=MESH)

    def send_both(copy, q, bs):
        @pl.when(has_up)
        def _():
            for b in bs:
                copy(q, b, True).start()

        @pl.when(has_down)
        def _():
            for b in bs:
                copy(q, b, False).start()

    def recv_both(copy, q, bs):
        @pl.when(has_down)
        def _():
            for b in bs:
                copy(q, b, True).wait_recv()

        @pl.when(has_up)
        def _():
            for b in bs:
                copy(q, b, False).wait_recv()

    def sent_all(copy):
        def body(b, carry):
            for q in range(2):
                @pl.when(has_up)
                def _():
                    copy(q, b, True).wait_send()

                @pl.when(has_down)
                def _():
                    copy(q, b, False).wait_send()
            return carry

        lax.fori_loop(0, blocks, body, 0)

    def over_chunks(f):
        def body(c, carry):
            f([c * PAIR + i for i in range(PAIR)])
            return carry

        lax.fori_loop(0, chunks, body, 0)

    def lane_pair(j):
        return 2 * j + 1, (2 * j + 2) % tiles

    def flat_rows(j, v):
        return pl.ds(starts[j] + v * fine, fine)

    def both_pieces(x):
        high, low = split(x)
        return jnp.concatenate([high, low], axis=1)

    def lift(g, b):
        pieces = []
        for i in range(3):
            if g < 2:
                pieces.append(halo[i, b, pl.ds(g * seg, seg), :])
            else:
                first = halo[i, b, pl.ds(0, seg), :]
                tail = halo[i, b, tail_rows, :]
                pieces.append(jnp.where(left, tail, swap(first[:half])))
                pieces.append(jnp.where(left, swap(tail), swap(first[half:])))
        wide = dot(rows_up[...], both_pieces(jnp.concatenate(pieces, axis=0)))
        return both_pieces(wide[:, :LANES] + wide[:, LANES:])

    def accumulate(j, bs, fields):
        for h, t in enumerate(lane_pair(j)):
            for v in range(n_vars):
                total = acc[h, flat_rows(j, v), :]
                for b, field in zip(bs, fields):
                    f = field[:, h * LANES:(h + 1) * LANES].reshape(GROUP, fine, LANES)
                    p = pert[pl.ds(b * GROUP, GROUP), v, :, t * LANES:(t + 1) * LANES]
                    total = total + jnp.sum(p * f, axis=0)
                acc[h, flat_rows(j, v), :] = total

    def forward_first(bs):
        recv_both(g_copy, 0, bs)
        new = [lift(0, b) for b in bs]
        for b, value in zip(bs, new):
            lifted[b] = value
        accumulate(0, bs, [dot(value, narrow_up[...]) for value in new])

    def odd_tile(a, b):
        return dot(a, wide_up[:2 * LANES, :]) + dot(b, wide_up[2 * LANES:, :])

    def forward_second(b, split_at=None):
        recv_both(g_copy, 1, [b])
        one, two = lift(1, b), lift(2, b)
        accumulate(1, [b], [odd_tile(lifted[b], one)])
        accumulate(2, [b], [dot(one, narrow_up[...])])
        if split_at is not None:
            split_at()
        accumulate(3, [b], [odd_tile(one, two)])
        accumulate(4, [b], [dot(two, narrow_up[...])])

    def weighted(j, b):
        pieces = []
        for h, t in enumerate(lane_pair(j)):
            total = None
            for v in range(n_vars):
                p = pert[pl.ds(b * GROUP, GROUP), v, :, t * LANES:(t + 1) * LANES]
                term = p * misfit[h, flat_rows(j, v), :][None]
                total = term if total is None else total + term
            pieces.append(split(total.reshape(GROUP * fine, LANES)))
        lhs = jnp.concatenate([pieces[0][0], pieces[1][0], pieces[0][1], pieces[1][1]], axis=1)
        return dot(lhs, narrow_down[...] if j % 2 == 0 else wide_down[...])

    def lower(x):
        wide = dot(rows_down[...], both_pieces(x))
        return (wide[:, :LANES] + wide[:, LANES:]) * (1.0 / SCALE)

    def keep(b, rows, coarse):
        part_send[0, b, rows, :] = coarse[0]
        own[b, rows, :] = coarse[1]
        part_send[1, b, rows, :] = coarse[2]

    def three(x):
        return x[:seg], x[seg:2 * seg], x[2 * seg:]

    def adjoint_first(bs):
        for b in bs:
            last = weighted(4, b)
            wide = weighted(1, b)
            wrapped = jnp.where(lax.broadcasted_iota(jnp.int32, last.shape, 1) < LANES // 2, swap(last), 0.0)
            first = weighted(0, b) + wide[:, :LANES] + wrapped
            spare[b, 0] = wide[:, LANES:]
            spare[b, 1] = last
            keep(b, pl.ds(0, seg), three(lower(first)))
        send_both(c_copy, 0, bs)

    def adjoint_second(bs):
        for b in bs:
            wide = weighted(3, b)
            keep(b, pl.ds(seg, seg), three(lower(spare[b, 0] + weighted(2, b) + wide[:, :LANES])))
            ends = three(lower(spare[b, 1] + wide[:, LANES:]))
            keep(b, tail_rows, [jnp.where(left, e[:half], swap(e[half:])) for e in ends])
        send_both(c_copy, 1, bs)

    def region(s):
        return pl.ds(bases[s], n_z * parts[s])

    def part_rows(s, at):
        return pl.ds(pl.multiple_of(bases[s] + at * parts[s], 8), parts[s])

    def pair_copy(s):
        return pltpu.make_async_remote_copy(
            src_ref=acc.at[1 - core, region(s)], dst_ref=pair_recv.at[region(s)],
            send_sem=p_ss.at[s], recv_sem=p_rs.at[s], device_id=partner, device_id_type=MESH)

    def z_copy(s, k):
        return pltpu.make_async_remote_copy(
            src_ref=half_sum.at[part_rows(s, lax.rem(z + k + 1, n_z))], dst_ref=z_recv.at[k, pl.ds(z_bases[s], parts[s])],
            send_sem=z_ss.at[s, k], recv_sem=z_rs.at[s, k], device_id=z_peers[k], device_id_type=MESH)

    def ag_copy(s, k, source):
        return pltpu.make_async_remote_copy(
            src_ref=image.at[core, part_rows(s, source)], dst_ref=image.at[core, part_rows(s, source)],
            send_sem=ag_ss.at[s, k], recv_sem=ag_rs.at[s, k], device_id=z_peers[k], device_id_type=MESH)

    def image_copy(index):
        return pltpu.make_async_remote_copy(
            src_ref=image.at[index], dst_ref=image.at[index],
            send_sem=im_ss.at[0], recv_sem=im_rs.at[0], device_id=partner, device_id_type=MESH)

    def pair_finish(s):
        pair_copy(s).wait_recv()
        half_sum[region(s), :] = acc[core, region(s), :] + pair_recv[region(s), :]
        for k in range(n_z - 1):
            z_copy(s, k).start()

    def z_finish(s):
        for k in range(n_z - 1):
            z_copy(s, k).wait_recv()
        total = half_sum[part_rows(s, z), :]
        for k in range(n_z - 1):
            total = total + z_recv[k, pl.ds(z_bases[s], parts[s]), :]
        total = total * (1.0 / SCALE)
        image[core, part_rows(s, z), :] = total
        if s < 2:
            gather_start(s)
        return total_of(total * total)

    def gather_start(s):
        for k in range(n_z - 1):
            ag_copy(s, k, z).start()

    def gather_pass():
        for s in range(3):
            for k in range(n_z - 1):
                ag_copy(s, k, lax.rem(z + n_z - 1 - k, n_z)).wait_recv()
        image_copy(core).start()

    def gather_finish():
        image_copy(1 - core).wait_recv()
        image_copy(core).wait_send()
        for s in range(3):
            pair_copy(s).wait_send()
            for k in range(n_z - 1):
                z_copy(s, k).wait_send()
                ag_copy(s, k, z).wait_send()

    def total_of(squares):
        return jnp.sum(squares.reshape(-1, 8, LANES), axis=0)

    def forward_all():
        acc[...] = jnp.zeros_like(acc)
        over_chunks(forward_first)
        pair_copy(0).start()

        def body(b, carry):
            forward_second(b)
            return carry

        forward_second(0)
        pair_finish(0)
        lax.fori_loop(1, blocks - 1, body, 0)
        forward_second(blocks - 1, lambda: pair_copy(1).start())
        pair_copy(2).start()
        pair_finish(1)
        pair_finish(2)
        squares = z_finish(0)
        squares = squares + z_finish(1)
        squares = squares + z_finish(2)
        return squares

    def sl_copy(it, k):
        return pltpu.make_async_remote_copy(
            src_ref=lat_send, dst_ref=lat_recv.at[it, k],
            send_sem=sl_ss.at[it, k], recv_sem=sl_rs.at[it, k], device_id=lat_peers[k], device_id_type=MESH)

    def sm_copy(it, k):
        return pltpu.make_async_remote_copy(
            src_ref=mem_send, dst_ref=mem_recv.at[it, k],
            send_sem=sm_ss.at[it, k], recv_sem=sm_rs.at[it, k], device_id=mem_peers[k], device_id_type=MESH)

    loads[0].wait()
    for b in range(blocks):
        block = control[:, pl.ds(b * GROUP, GROUP), :].reshape(seg, control.shape[2])
        ends = block[:, 2 * LANES:]
        tail = jnp.concatenate([ends[:half], ends[half:]], axis=1)
        for rows, value in ((pl.ds(0, seg), block[:, :LANES]), (pl.ds(seg, seg), block[:, LANES:2 * LANES]), (pl.ds(2 * seg, half), tail)):
            halo[1, b, rows, :] = value
            w[b, rows, :] = value

    pl.semaphore_wait(barrier, len(lat_peers) + len(mem_peers))
    over_chunks(functools.partial(send_both, g_copy, 0))
    over_chunks(functools.partial(send_both, g_copy, 1))

    zero = jnp.zeros(halo.shape[2:], jnp.float32)

    @pl.when(jnp.logical_not(has_up))
    def _():
        for b in range(blocks):
            halo[0, b] = zero
            part_recv[1, b] = zero

    @pl.when(jnp.logical_not(has_down))
    def _():
        for b in range(blocks):
            halo[2, b] = zero
            part_recv[0, b] = zero

    for load in loads[1:]:
        load.wait()
    for j in range(pairs):
        for h, t in enumerate(lane_pair(j)):
            for v in range(n_vars):
                obs[h, flat_rows(j, v), :] = innov[v, :, t * LANES:(t + 1) * LANES]
    for c in range(blocks):
        pert_copy(c).wait()

    def widen(m, carry):
        pert[m] = pert_raw[m].astype(jnp.float32)
        return carry

    lax.fori_loop(0, pert.shape[0], widen, 0)
    forward_all()
    gather_start(2)
    sent_all(g_copy)
    gather_pass()
    gather_finish()
    inc[...] = image[...]

    def step(it, carry):
        for h in range(2):
            for j in range(pairs):
                for v in range(n_vars):
                    rows = flat_rows(j, v)
                    misfit[h, rows, :] = jnp.clip(inc[h, rows, :] - obs[h, rows, :], -thr[v], thr[v])
        over_chunks(adjoint_first)
        over_chunks(adjoint_second)

        def gradient(q):
            def body(b, squares):
                recv_both(c_copy, q, [b])
                rows = pl.ds(*groups[q])
                grad = w[b, rows, :] + own[b, rows, :] + part_recv[0, b, rows, :] + part_recv[1, b, rows, :]
                halo[1, b, rows, :] = grad
                send_both(g_copy, q, [b])
                return squares + total_of(grad * grad)

            return lax.fori_loop(0, blocks, body, jnp.zeros((8, LANES), jnp.float32))

        grad_sq = gradient(0)
        grad_sq = grad_sq + gradient(1)
        image_sq = forward_all()
        sums = jnp.concatenate([jnp.sum(grad_sq, axis=0, keepdims=True), jnp.sum(image_sq, axis=0, keepdims=True)], axis=0)
        lat_send[...] = sums
        for k in range(n_lat - 1):
            sl_copy(it, k).start()
        gather_start(2)
        sent_all(c_copy)
        sent_all(g_copy)
        gather_pass()
        for k in range(n_lat - 1):
            sl_copy(it, k).wait_recv()
        sums = sums + jnp.sum(lat_recv[it], axis=0)
        mem_send[...] = sums
        for k in range(n_mem - 1):
            sm_copy(it, k).start()
        for k in range(n_lat - 1):
            sl_copy(it, k).wait_send()
        gather_finish()
        for k in range(n_mem - 1):
            sm_copy(it, k).wait_recv()
        sums = sums + jnp.sum(mem_recv[it], axis=0)
        g2 = jnp.sum(sums[0:1, :], axis=1, keepdims=True)
        h2 = jnp.sum(sums[1:2, :], axis=1, keepdims=True)
        step_len = g2 / (g2 + h2)
        inc[...] = inc[...] - step_len[None] * image[...]
        for b in range(blocks):
            w[b] = w[b] - step_len * halo[1, b]
        for k in range(n_mem - 1):
            sm_copy(it, k).wait_send()
        return carry

    lax.fori_loop(0, STEPS, step, 0)

    for b in range(blocks):
        members = pl.ds(b * GROUP, GROUP)
        tail = w[b, pl.ds(2 * seg, half), :]
        weights_out[:, members, :LANES] = w[b, pl.ds(0, seg), :].reshape(n_rows, GROUP, LANES)
        weights_out[:, members, LANES:2 * LANES] = w[b, pl.ds(seg, seg), :].reshape(n_rows, GROUP, LANES)
        weights_out[:n_rows // 2, members, 2 * LANES:] = tail[:, :LANES // 2].reshape(n_rows // 2, GROUP, LANES // 2)
        weights_out[n_rows // 2:, members, 2 * LANES:] = tail[:, LANES // 2:].reshape(n_rows // 2, GROUP, LANES // 2)

    share = inc_out.shape[2]
    first = mem * share // LANES
    shift = mem * share - first * LANES

    def lane_tile(t, v):
        j = jnp.where(t % 2 == 1, (t - 1) // 2, (t // 2 + pairs - 1) % pairs)
        row = jnp.int32(0)
        for i in range(pairs):
            row = jnp.where(j == i, starts[i] + v * fine, row)
        return inc[1 - t % 2, pl.ds(pl.multiple_of(row, 8), fine), :]

    fine_lane = lax.broadcasted_iota(jnp.int32, (fine, LANES), 1)
    for v in range(n_vars):
        a = pltpu.roll(lane_tile(first, v), (LANES - shift) % LANES, 1)
        b = pltpu.roll(lane_tile(first + 1, v), (LANES - shift) % LANES, 1)
        inc_out[v, :, :LANES] = jnp.where(fine_lane < LANES - shift, a, b)
        inc_out[v, :, LANES:] = b[:, :share - LANES]


def per_device(n_mem, n_lat, perturbations, control, innovations, thresholds):
    members, coarse_rows, coarse_cols = control.shape
    n_vars, fine_rows, fine_cols = innovations.shape
    blocks = members // GROUP
    seg = GROUP * coarse_rows
    packed = seg * coarse_cols // LANES
    n_z = n_mem // 2
    tile_rows = n_vars * fine_rows
    pairs = fine_cols // (2 * LANES)
    parts, bases, starts, flat = [], [], [], 0
    for count in (1, 2, pairs - 3):
        parts.append(-(-count * tile_rows // n_z // 8) * 8)
        bases.append(flat)
        starts += [flat + i * tile_rows for i in range(count)]
        flat += n_z * parts[-1]
    vmem = pl.BlockSpec(memory_space=pltpu.VMEM)
    whole = pl.BlockSpec(memory_space=pl.ANY)
    f32 = jnp.float32
    bf16 = jnp.bfloat16
    dma = pltpu.SemaphoreType.DMA
    constants = tables(coarse_rows)
    ordered = control.transpose(1, 0, 2)
    shapes = (
        jax.ShapeDtypeStruct(ordered.shape, f32),
        jax.ShapeDtypeStruct((n_vars, fine_rows, fine_cols // n_mem), f32))
    weights, increment = pl.pallas_call(
        functools.partial(kernel, n_mem, n_lat, seg, (bases, parts, starts)),
        out_shape=tuple(pltpu.VMEM(x.shape, f32) for x in shapes),
        in_specs=[whole, whole, whole, pl.BlockSpec(memory_space=pltpu.SMEM)] + [whole] * 6,
        out_specs=(vmem, vmem),
        scratch_shapes=[
            pltpu.VMEM(perturbations.shape, bf16),
            pltpu.VMEM(perturbations.shape, f32),
            pltpu.VMEM(ordered.shape, f32),
            pltpu.VMEM(innovations.shape, f32),
            pltpu.VMEM(constants[0].shape[1:], bf16),
            pltpu.VMEM(constants[1].shape[1:], bf16),
            pltpu.VMEM(constants[2].shape, bf16),
            pltpu.VMEM(constants[3].shape, bf16),
            pltpu.VMEM(constants[4].shape, bf16),
            pltpu.VMEM(constants[5].shape, bf16),
            pltpu.VMEM((3, blocks, packed, LANES), f32),
            pltpu.VMEM((2, blocks, packed, LANES), f32),
            pltpu.VMEM((2, blocks, packed, LANES), f32),
            pltpu.VMEM((blocks, packed, LANES), f32),
            pltpu.VMEM((blocks, packed, LANES), f32),
            pltpu.VMEM((blocks, 2, GROUP * fine_rows, LANES), f32),
            pltpu.VMEM((blocks, GROUP * fine_rows, 2 * LANES), bf16),
            pltpu.VMEM((2, flat, LANES), f32),
            pltpu.VMEM((flat, LANES), f32),
            pltpu.VMEM((flat, LANES), f32),
            pltpu.VMEM((n_z - 1, sum(parts), LANES), f32),
            pltpu.VMEM((2, flat, LANES), f32),
            pltpu.VMEM((2, flat, LANES), f32),
            pltpu.VMEM((2, flat, LANES), f32),
            pltpu.VMEM((2, flat, LANES), f32),
            pltpu.VMEM((2, LANES), f32),
            pltpu.VMEM((STEPS, n_lat - 1, 2, LANES), f32),
            pltpu.VMEM((2, LANES), f32),
            pltpu.VMEM((STEPS, n_mem - 1, 2, LANES), f32),
            dma((blocks,)), dma((8,)),
            dma((2, 2, blocks)), dma((2, 2, blocks)), dma((2, 2, blocks)), dma((2, 2, blocks)),
            dma((3,)), dma((3,)), dma((3, n_z - 1)), dma((3, n_z - 1)), dma((3, n_z - 1)), dma((3, n_z - 1)), dma((1,)), dma((1,)),
            dma((STEPS, n_lat - 1)), dma((STEPS, n_lat - 1)), dma((STEPS, n_mem - 1)), dma((STEPS, n_mem - 1)),
        ],
        compiler_params=pltpu.CompilerParams(collective_id=0, has_side_effects=True),
    )(perturbations, ordered, innovations, thresholds, *constants)
    return weights.transpose(1, 0, 2), increment


def solution(mesh):
    return jax.shard_map(
        functools.partial(per_device, mesh.shape["mem"], mesh.shape["lat"]),
        mesh=mesh,
        in_specs=(P("mem", None, "lat", None), P("mem", "lat", None), P(None, "lat", None), P()),
        out_specs=(P("mem", "lat", None), P(None, "lat", "mem")),
        check_vma=False,
    )
```

time: 618 us -> 90 us (0.15); the launches traced: 608 us -> 88.9 us
  waiting for transfers between devices: 246 us -> 0 us
  blocking collectives: 207 us -> 0 us
  Pallas kernels: 0 us -> 87 us
  starting transfers between devices: 63.1 us -> 0 us
  matrix products: 48.9 us -> 0 us
  other arithmetic: 22.3 us -> 0 us
  between operations: 18.6 us -> 0.64 us
    psum x4 -> x0, blocking collectives: 207 us -> none  [the longest x2 130 us: per_device(): grad_sq = lax.psum(jnp.sum(gradient * gradient), ('mem', 'lat'))]
    psum x3 -> x0, waiting for transfers between devices: 205 us -> none  [combine_members(): return lax.psum(partial_value, 'mem')]
    pallas_call x0 -> x1, Pallas kernels: none -> 87 us  [per_device(): pl.pallas_call(functools.partial(kernel, n_mem, n_lat, seg, (bases, parts...]
    ppermute x20 -> x0, starting transfers between devices: 62.5 us -> none  [the longest x10 49.2 us: with_halo(): lax.ppermute(tail, axis, [(i, (i + 1) % count) for i in range(ends)])]
    dot_general x15 -> x0, matrix products: 48.9 us -> none  [the longest x3 23.1 us: forward(): jnp.dot(rowwise.reshape(members * fine_rows, coarse_cols), lon_up, precis...]
    ppermute x20 -> x0, waiting for transfers between devices: 41.4 us -> none  [the longest x10 26.2 us: with_halo(): lax.ppermute(head, axis, [((i + 1) % count, i) for i in range(ends)])]
    reduce_sum x7 -> x0, other arithmetic: 18.2 us -> none  [the longest x2 8.98 us: per_device(): weighted = jnp.sum(perturbations.astype(jnp.float32) * misfit[None], axis=1)]
  transfers between devices with their start and end apart: 23 -> 0, of which waited for: 21 -> 0; matrix products, arithmetic and copies ran while one was open for 0% -> 0% of each run, Pallas kernels for 0% -> 0%
where the time goes in v2:
time: 90 us; the launch traced here: 88.9 us
  Pallas kernels  87 us (97%)
  local copies, waits for them, and re-layouts  1.35 us (2%)
    pallas_call x1, Pallas kernels, per_device(): pl.pallas_call(functools.partial(kernel, n_mem, n_lat, seg, (bases, parts...  87 us

profile of v2, /device:TPU:0, one launch (start us, length us, event | category | flops | bytes accessed | tf_op | source)
XLA Modules:
  0.0 88.9 jit_solution(9510005405517574298)
XLA Ops:
  0.6 87.0 %shard_map.113 = (f32[6,32,320]{2,1,0:T(8,128)S(1)}, f32[3,24,160]{2,1,0:T(8,128)S(1)}) custom-call(bf16[32,3,24,1280]{3,2,1,0:T(8,128)(2,1)} %pert_hbm.1, f32[6,32,320]{2,1,0:T(8,128)} %bitcast.3, f32[3,24,1280]{2,1,0:T(8,128)} %innov_hbm.1, f32[3]{0:T(128)} %thr.1, bf16[3,192,144]{2,1,0:T(8,128)(2,1)} %constant.12.clone.rows_up_hbm, ...), custom_call_target="tpu_custom_call" | custom-call | tf_op jit(solution)/shard_map/pallas_call | solution.py:542
  87.6 0.7 copy.14
  88.3 0.6 copy.15

commit v3 on v2

--- a/solution.py
+++ b/solution.py
@@ -11,6 +11,7 @@
 RATIO = 4
 HALF = 5
 STEPS = 2
+SIDE = 4
 GROUP = 8
 PAIR = 2
 LANES = 128
@@ -97,10 +98,11 @@
     has_down = lat < n_lat - 1
     partner = (2 * z + 1 - core, lat)
     z_peers = [(2 * lax.rem(z + k, n_z) + core, lat) for k in range(1, n_z)]
-    mem_peers = [(lax.rem(mem + k, n_mem), lat) for k in range(1, n_mem)]
-    lat_peers = [(mem, lax.rem(lat + k, n_lat)) for k in range(1, n_lat)]
-    groups = ((0, seg), (seg, seg + half))
-    tail_rows = pl.ds(2 * seg, half)
+    mem_peers = [(2 * lax.rem(z + k, n_z) + c, lat) for k in (2, 1, 3) for c in (core, 1 - core)] + [partner]
+    far = sorted(((i, k) for i in range(SIDE) for k in range(SIDE) if i or k), key=lambda at: -sum(min(d, SIDE - d) for d in at))
+    lat_peers = [(mem, lax.rem(lat // SIDE + i, SIDE) * SIDE + lax.rem(lat + k, SIDE)) for i, k in far]
+    groups = ((0, seg + half), (seg + half, seg))
+    first_rows, tail_rows, second_rows = pl.ds(0, seg), pl.ds(seg, half), pl.ds(seg + half, seg)
     bases, parts, starts = layout
     z_bases = [sum(parts[:i]) for i in range(3)]
 
@@ -205,9 +207,9 @@
         pieces = []
         for i in range(3):
             if g < 2:
-                pieces.append(halo[i, b, pl.ds(g * seg, seg), :])
+                pieces.append(halo[i, b, second_rows if g else first_rows, :])
             else:
-                first = halo[i, b, pl.ds(0, seg), :]
+                first = halo[i, b, first_rows, :]
                 tail = halo[i, b, tail_rows, :]
                 pieces.append(jnp.where(left, tail, swap(first[:half])))
                 pieces.append(jnp.where(left, swap(tail), swap(first[half:])))
@@ -226,23 +228,25 @@
 
     def forward_first(bs):
         recv_both(g_copy, 0, bs)
-        new = [lift(0, b) for b in bs]
-        for b, value in zip(bs, new):
-            lifted[b] = value
-        accumulate(0, bs, [dot(value, narrow_up[...]) for value in new])
+        zero_th = [lift(0, b) for b in bs]
+        two = [lift(2, b) for b in bs]
+        for b, p, q in zip(bs, zero_th, two):
+            lifted[b, 0] = p
+            lifted[b, 1] = q
+        accumulate(0, bs, [dot(value, narrow_up[...]) for value in zero_th])
+        accumulate(4, bs, [dot(value, narrow_up[...]) for value in two])
 
     def odd_tile(a, b):
         return dot(a, wide_up[:2 * LANES, :]) + dot(b, wide_up[2 * LANES:, :])
 
     def forward_second(b, split_at=None):
         recv_both(g_copy, 1, [b])
-        one, two = lift(1, b), lift(2, b)
-        accumulate(1, [b], [odd_tile(lifted[b], one)])
+        one = lift(1, b)
+        accumulate(1, [b], [odd_tile(lifted[b, 0], one)])
         accumulate(2, [b], [dot(one, narrow_up[...])])
         if split_at is not None:
             split_at()
-        accumulate(3, [b], [odd_tile(one, two)])
-        accumulate(4, [b], [dot(two, narrow_up[...])])
+        accumulate(3, [b], [odd_tile(one, lifted[b, 1])])
 
     def weighted(j, b):
         pieces = []
@@ -272,19 +276,18 @@
         for b in bs:
             last = weighted(4, b)
             wide = weighted(1, b)
+            high = weighted(3, b)
             wrapped = jnp.where(lax.broadcasted_iota(jnp.int32, last.shape, 1) < LANES // 2, swap(last), 0.0)
             first = weighted(0, b) + wide[:, :LANES] + wrapped
-            spare[b, 0] = wide[:, LANES:]
-            spare[b, 1] = last
-            keep(b, pl.ds(0, seg), three(lower(first)))
+            spare[b] = wide[:, LANES:] + high[:, :LANES]
+            keep(b, first_rows, three(lower(first)))
+            ends = three(lower(last + high[:, LANES:]))
+            keep(b, tail_rows, [jnp.where(left, e[:half], swap(e[half:])) for e in ends])
         send_both(c_copy, 0, bs)
 
     def adjoint_second(bs):
         for b in bs:
-            wide = weighted(3, b)
-            keep(b, pl.ds(seg, seg), three(lower(spare[b, 0] + weighted(2, b) + wide[:, :LANES])))
-            ends = three(lower(spare[b, 1] + wide[:, LANES:]))
-            keep(b, tail_rows, [jnp.where(left, e[:half], swap(e[half:])) for e in ends])
+            keep(b, second_rows, three(lower(spare[b] + weighted(2, b))))
         send_both(c_copy, 1, bs)
 
     def region(s):
@@ -362,9 +365,8 @@
             forward_second(b)
             return carry
 
-        forward_second(0)
+        lax.fori_loop(0, blocks - 1, body, 0)
         pair_finish(0)
-        lax.fori_loop(1, blocks - 1, body, 0)
         forward_second(blocks - 1, lambda: pair_copy(1).start())
         pair_copy(2).start()
         pair_finish(1)
@@ -389,7 +391,7 @@
         block = control[:, pl.ds(b * GROUP, GROUP), :].reshape(seg, control.shape[2])
         ends = block[:, 2 * LANES:]
         tail = jnp.concatenate([ends[:half], ends[half:]], axis=1)
-        for rows, value in ((pl.ds(0, seg), block[:, :LANES]), (pl.ds(seg, seg), block[:, LANES:2 * LANES]), (pl.ds(2 * seg, half), tail)):
+        for rows, value in ((first_rows, block[:, :LANES]), (second_rows, block[:, LANES:2 * LANES]), (tail_rows, tail)):
             halo[1, b, rows, :] = value
             w[b, rows, :] = value
 
@@ -438,7 +440,8 @@
                 for v in range(n_vars):
                     rows = flat_rows(j, v)
                     misfit[h, rows, :] = jnp.clip(inc[h, rows, :] - obs[h, rows, :], -thr[v], thr[v])
-        over_chunks(adjoint_first)
+        for bs in ((0,), (1,), (2, 3)):
+            adjoint_first(bs)
         over_chunks(adjoint_second)
 
         def gradient(q):
@@ -489,9 +492,9 @@
 
     for b in range(blocks):
         members = pl.ds(b * GROUP, GROUP)
-        tail = w[b, pl.ds(2 * seg, half), :]
-        weights_out[:, members, :LANES] = w[b, pl.ds(0, seg), :].reshape(n_rows, GROUP, LANES)
-        weights_out[:, members, LANES:2 * LANES] = w[b, pl.ds(seg, seg), :].reshape(n_rows, GROUP, LANES)
+        tail = w[b, tail_rows, :]
+        weights_out[:, members, :LANES] = w[b, first_rows, :].reshape(n_rows, GROUP, LANES)
+        weights_out[:, members, LANES:2 * LANES] = w[b, second_rows, :].reshape(n_rows, GROUP, LANES)
         weights_out[:n_rows // 2, members, 2 * LANES:] = tail[:, :LANES // 2].reshape(n_rows // 2, GROUP, LANES // 2)
         weights_out[n_rows // 2:, members, 2 * LANES:] = tail[:, LANES // 2:].reshape(n_rows // 2, GROUP, LANES // 2)
 
@@ -523,11 +526,13 @@
     n_z = n_mem // 2
     tile_rows = n_vars * fine_rows
     pairs = fine_cols // (2 * LANES)
-    parts, bases, starts, flat = [], [], [], 0
-    for count in (1, 2, pairs - 3):
-        parts.append(-(-count * tile_rows // n_z // 8) * 8)
+    parts, bases, flat = [], [], 0
+    starts = [0] * pairs
+    for tiles in ((0, 4), (1, 2), (3,)):
+        parts.append(-(-len(tiles) * tile_rows // n_z // 8) * 8)
         bases.append(flat)
-        starts += [flat + i * tile_rows for i in range(count)]
+        for i, j in enumerate(tiles):
+            starts[j] = flat + i * tile_rows
         flat += n_z * parts[-1]
     vmem = pl.BlockSpec(memory_space=pltpu.VMEM)
     whole = pl.BlockSpec(memory_space=pl.ANY)
@@ -560,8 +565,8 @@
             pltpu.VMEM((2, blocks, packed, LANES), f32),
             pltpu.VMEM((blocks, packed, LANES), f32),
             pltpu.VMEM((blocks, packed, LANES), f32),
-            pltpu.VMEM((blocks, 2, GROUP * fine_rows, LANES), f32),
-            pltpu.VMEM((blocks, GROUP * fine_rows, 2 * LANES), bf16),
+            pltpu.VMEM((blocks, GROUP * fine_rows, LANES), f32),
+            pltpu.VMEM((blocks, 2, GROUP * fine_rows, 2 * LANES), bf16),
             pltpu.VMEM((2, flat, LANES), f32),
             pltpu.VMEM((flat, LANES), f32),
             pltpu.VMEM((flat, LANES), f32),

time: 90 us -> 89.1 us (0.990)
  Pallas kernels: 87 us -> 86 us
    pallas_call x1, Pallas kernels: 87 us -> 86 us  [per_device(): pl.pallas_call(functools.partial(kernel, n_mem, n_lat, seg, (bases, parts...]
where the time goes in v3:
time: 89.1 us; the launch traced here: 88 us
  Pallas kernels  86 us (97%)
  local copies, waits for them, and re-layouts  1.35 us (2%)
    pallas_call x1, Pallas kernels, per_device(): pl.pallas_call(functools.partial(kernel, n_mem, n_lat, seg, (bases, parts...  86 us

profile of v3, /device:TPU:0, one launch (start us, length us, event | category | flops | bytes accessed | tf_op | source)
XLA Modules:
  0.0 88.0 jit_solution(6730287428259058493)
XLA Ops:
  0.6 86.0 %shard_map.113 = (f32[6,32,320]{2,1,0:T(8,128)S(1)}, f32[3,24,160]{2,1,0:T(8,128)S(1)}) custom-call(bf16[32,3,24,1280]{3,2,1,0:T(8,128)(2,1)} %pert_hbm.1, f32[6,32,320]{2,1,0:T(8,128)} %bitcast.3, f32[3,24,1280]{2,1,0:T(8,128)} %innov_hbm.1, f32[3]{0:T(128)} %thr.1, bf16[3,192,144]{2,1,0:T(8,128)(2,1)} %constant.12.clone.rows_up_hbm, ...), custom_call_target="tpu_custom_call" | custom-call | tf_op jit(solution)/shard_map/pallas_call | solution.py:547
  86.6 0.7 copy.14
  87.4 0.6 copy.15

commit v4 on v3

--- a/solution.py
+++ b/solution.py
@@ -70,9 +70,9 @@
 
 def kernel(
     n_mem, n_lat, seg, layout,
-    pert_hbm, control_hbm, innov_hbm, thr, rows_up_hbm, rows_down_hbm, narrow_up_hbm, wide_up_hbm, narrow_down_hbm, wide_down_hbm,
+    pert_hbm, control_hbm, innov_hbm, thr_hbm, rows_up_hbm, rows_down_hbm, narrow_up_hbm, wide_up_hbm, narrow_down_hbm, wide_down_hbm,
     weights_out, inc_out,
-    pert_raw, pert, control, innov, rows_up, rows_down, narrow_up, wide_up, narrow_down, wide_down,
+    thr, pert_raw, pert, control, innov, rows_up, rows_down, narrow_up, wide_up, narrow_down, wide_down,
     halo, part_send, part_recv, own, w, spare, lifted, acc, pair_recv, half_sum, z_recv, image, inc, misfit, obs,
     lat_send, lat_recv, mem_send, mem_recv,
     pert_sem, load_sem, g_send, g_recv, c_send, c_recv, p_ss, p_rs, z_ss, z_rs, ag_ss, ag_rs, im_ss, im_rs, sl_ss, sl_rs, sm_ss, sm_rs,
@@ -109,6 +109,7 @@
     loads = [
         (control_hbm, control), (rows_up_hbm.at[case], rows_up), (narrow_up_hbm, narrow_up), (wide_up_hbm, wide_up),
         (innov_hbm, innov), (rows_down_hbm.at[case], rows_down), (narrow_down_hbm, narrow_down), (wide_down_hbm, wide_down),
+        (thr_hbm, thr),
     ]
     loads = [pltpu.make_async_copy(src, dst, load_sem.at[i]) for i, (src, dst) in enumerate(loads)]
 
@@ -434,15 +435,19 @@
     gather_finish()
     inc[...] = image[...]
 
-    def step(it, carry):
+    def step(it, step_len):
         for h in range(2):
-            for j in range(pairs):
+            for j in (4, 0, 1, 3, 2):
                 for v in range(n_vars):
                     rows = flat_rows(j, v)
-                    misfit[h, rows, :] = jnp.clip(inc[h, rows, :] - obs[h, rows, :], -thr[v], thr[v])
+                    moved = inc[h, rows, :] - step_len * image[h, rows, :]
+                    inc[h, rows, :] = moved
+                    misfit[h, rows, :] = jnp.clip(moved - obs[h, rows, :], -thr[v], thr[v])
         for bs in ((0,), (1,), (2, 3)):
             adjoint_first(bs)
         over_chunks(adjoint_second)
+        for b in range(blocks):
+            w[b] = w[b] - step_len * halo[1, b]
 
         def gradient(q):
             def body(b, squares):
@@ -459,42 +464,40 @@
         grad_sq = grad_sq + gradient(1)
         image_sq = forward_all()
         sums = jnp.concatenate([jnp.sum(grad_sq, axis=0, keepdims=True), jnp.sum(image_sq, axis=0, keepdims=True)], axis=0)
+        mem_send[...] = sums
+        for k in range(n_mem - 1):
+            sm_copy(it, k).start()
+        gather_start(2)
+        sent_all(c_copy)
+        sent_all(g_copy)
+        for k in range(n_mem - 1):
+            sm_copy(it, k).wait_recv()
+        sums = sums + jnp.sum(mem_recv[it], axis=0)
         lat_send[...] = sums
         for k in range(n_lat - 1):
             sl_copy(it, k).start()
-        gather_start(2)
-        sent_all(c_copy)
-        sent_all(g_copy)
         gather_pass()
+        gather_finish()
         for k in range(n_lat - 1):
             sl_copy(it, k).wait_recv()
         sums = sums + jnp.sum(lat_recv[it], axis=0)
-        mem_send[...] = sums
-        for k in range(n_mem - 1):
-            sm_copy(it, k).start()
         for k in range(n_lat - 1):
             sl_copy(it, k).wait_send()
-        gather_finish()
-        for k in range(n_mem - 1):
-            sm_copy(it, k).wait_recv()
-        sums = sums + jnp.sum(mem_recv[it], axis=0)
         g2 = jnp.sum(sums[0:1, :], axis=1, keepdims=True)
         h2 = jnp.sum(sums[1:2, :], axis=1, keepdims=True)
         step_len = g2 / (g2 + h2)
-        inc[...] = inc[...] - step_len[None] * image[...]
-        for b in range(blocks):
-            w[b] = w[b] - step_len * halo[1, b]
         for k in range(n_mem - 1):
             sm_copy(it, k).wait_send()
-        return carry
-
-    lax.fori_loop(0, STEPS, step, 0)
+        return step_len
+
+    step_len = lax.fori_loop(0, STEPS, step, jnp.zeros((1, 1), jnp.float32))
 
     for b in range(blocks):
         members = pl.ds(b * GROUP, GROUP)
-        tail = w[b, tail_rows, :]
-        weights_out[:, members, :LANES] = w[b, first_rows, :].reshape(n_rows, GROUP, LANES)
-        weights_out[:, members, LANES:2 * LANES] = w[b, second_rows, :].reshape(n_rows, GROUP, LANES)
+        final = w[b] - step_len * halo[1, b]
+        one, tail, two = final[:seg], final[seg:seg + half], final[seg + half:]
+        weights_out[:, members, :LANES] = one.reshape(n_rows, GROUP, LANES)
+        weights_out[:, members, LANES:2 * LANES] = two.reshape(n_rows, GROUP, LANES)
         weights_out[:n_rows // 2, members, 2 * LANES:] = tail[:, :LANES // 2].reshape(n_rows // 2, GROUP, LANES // 2)
         weights_out[n_rows // 2:, members, 2 * LANES:] = tail[:, LANES // 2:].reshape(n_rows // 2, GROUP, LANES // 2)
 
@@ -507,7 +510,8 @@
         row = jnp.int32(0)
         for i in range(pairs):
             row = jnp.where(j == i, starts[i] + v * fine, row)
-        return inc[1 - t % 2, pl.ds(pl.multiple_of(row, 8), fine), :]
+        rows = pl.ds(pl.multiple_of(row, 8), fine)
+        return inc[1 - t % 2, rows, :] - step_len * image[1 - t % 2, rows, :]
 
     fine_lane = lax.broadcasted_iota(jnp.int32, (fine, LANES), 1)
     for v in range(n_vars):
@@ -547,9 +551,10 @@
     weights, increment = pl.pallas_call(
         functools.partial(kernel, n_mem, n_lat, seg, (bases, parts, starts)),
         out_shape=tuple(pltpu.VMEM(x.shape, f32) for x in shapes),
-        in_specs=[whole, whole, whole, pl.BlockSpec(memory_space=pltpu.SMEM)] + [whole] * 6,
+        in_specs=[whole] * 10,
         out_specs=(vmem, vmem),
         scratch_shapes=[
+            pltpu.SMEM(thresholds.shape, f32),
             pltpu.VMEM(perturbations.shape, bf16),
             pltpu.VMEM(perturbations.shape, f32),
             pltpu.VMEM(ordered.shape, f32),
@@ -579,7 +584,7 @@
             pltpu.VMEM((STEPS, n_lat - 1, 2, LANES), f32),
             pltpu.VMEM((2, LANES), f32),
             pltpu.VMEM((STEPS, n_mem - 1, 2, LANES), f32),
-            dma((blocks,)), dma((8,)),
+            dma((blocks,)), dma((9,)),
             dma((2, 2, blocks)), dma((2, 2, blocks)), dma((2, 2, blocks)), dma((2, 2, blocks)),
             dma((3,)), dma((3,)), dma((3, n_z - 1)), dma((3, n_z - 1)), dma((3, n_z - 1)), dma((3, n_z - 1)), dma((1,)), dma((1,)),
             dma((STEPS, n_lat - 1)), dma((STEPS, n_lat - 1)), dma((STEPS, n_mem - 1)), dma((STEPS, n_mem - 1)),

time: 89.1 us -> 87.7 us (0.984)
  no operation moved by 1% of the time
where the time goes in v4:
time: 87.7 us; the launch traced here: 87.5 us
  Pallas kernels  85.5 us (97%)
  local copies, waits for them, and re-layouts  1.35 us (2%)
    pallas_call x1, Pallas kernels, per_device(): pl.pallas_call(functools.partial(kernel, n_mem, n_lat, seg, (bases, parts...  85.5 us

profile of v4, /device:TPU:0, one launch (start us, length us, event | category | flops | bytes accessed | tf_op | source)
XLA Modules:
  0.0 87.5 jit_solution(16821079673267004474)
XLA Ops:
  0.6 85.5 %shard_map.113 = (f32[6,32,320]{2,1,0:T(8,128)S(1)}, f32[3,24,160]{2,1,0:T(8,128)S(1)}) custom-call(bf16[32,3,24,1280]{3,2,1,0:T(8,128)(2,1)} %pert_hbm.1, f32[6,32,320]{2,1,0:T(8,128)} %bitcast.3, f32[3,24,1280]{2,1,0:T(8,128)} %innov_hbm.1, f32[3]{0:T(128)} %thr_hbm.1, bf16[3,192,144]{2,1,0:T(8,128)(2,1)} %constant.12.clone.rows_up_hbm, ...), custom_call_target="tpu_custom_call" | custom-call | tf_op jit(solution)/shard_map/pallas_call | solution.py:551
  86.1 0.7 copy.14
  86.8 0.6 copy.15

commit v5 on v4

--- a/solution.py
+++ b/solution.py
@@ -443,7 +443,7 @@
                     moved = inc[h, rows, :] - step_len * image[h, rows, :]
                     inc[h, rows, :] = moved
                     misfit[h, rows, :] = jnp.clip(moved - obs[h, rows, :], -thr[v], thr[v])
-        for bs in ((0,), (1,), (2, 3)):
+        for bs in ((0,), (1,), (2,), (3,)):
             adjoint_first(bs)
         over_chunks(adjoint_second)
         for b in range(blocks):
@@ -519,6 +519,14 @@
         b = pltpu.roll(lane_tile(first + 1, v), (LANES - shift) % LANES, 1)
         inc_out[v, :, :LANES] = jnp.where(fine_lane < LANES - shift, a, b)
         inc_out[v, :, LANES:] = b[:, :share - LANES]
+
+
+def copy_kernel(a_ref, b_ref, c_ref, d_ref, sems):
+    copies = [pltpu.make_async_copy(a_ref, c_ref, sems.at[0]), pltpu.make_async_copy(b_ref, d_ref, sems.at[1])]
+    for copy in copies:
+        copy.start()
+    for copy in copies:
+        copy.wait()
 
 
 def per_device(n_mem, n_lat, perturbations, control, innovations, thresholds):
@@ -591,6 +599,9 @@
         ],
         compiler_params=pltpu.CompilerParams(collective_id=0, has_side_effects=True),
     )(perturbations, ordered, innovations, thresholds, *constants)
+    weights, increment = pl.pallas_call(
+        copy_kernel, out_shape=shapes, in_specs=[vmem] * 2, out_specs=(whole, whole),
+        scratch_shapes=[dma((2,))])(pltpu.with_memory_space_constraint(weights, pltpu.VMEM), pltpu.with_memory_space_constraint(increment, pltpu.VMEM))
     return weights.transpose(1, 0, 2), increment
 
 

time: 87.7 us -> 86.9 us (level)
  local copies, waits for them, and re-layouts: 1.35 us -> 0 us
    unnamed x2 -> x0, local copies, waits for them, and re-layouts: 1.35 us -> none
where the time goes in v5:
time: 86.9 us; the launch traced here: 86.7 us
  Pallas kernels  86 us (99%)
    pallas_call x1, Pallas kernels, per_device(): pl.pallas_call(functools.partial(kernel, n_mem, n_lat, seg, (bases, parts...  85.3 us

profile of v5, /device:TPU:0, one launch (start us, length us, event | category | flops | bytes accessed | tf_op | source)
XLA Modules:
  0.0 86.7 jit_solution(6785879912619360738)
XLA Ops:
  0.6 85.3 %shard_map.113 = (f32[6,32,320]{2,1,0:T(8,128)S(1)}, f32[3,24,160]{2,1,0:T(8,128)S(1)}) custom-call(bf16[32,3,24,1280]{3,2,1,0:T(8,128)(2,1)} %pert_hbm.1, f32[6,32,320]{2,1,0:T(8,128)} %bitcast.2, f32[3,24,1280]{2,1,0:T(8,128)} %innov_hbm.1, f32[3]{0:T(128)} %thr_hbm.1, bf16[3,192,144]{2,1,0:T(8,128)(2,1)} %constant.12.clone.rows_up_hbm, ...), custom_call_target="tpu_custom_call" | custom-call | tf_op jit(solution)/shard_map/pallas_call | solution.py:559
  85.9 0.7 shard_map.114

commit v6 on v5

--- a/solution.py
+++ b/solution.py
@@ -104,6 +104,7 @@
     groups = ((0, seg + half), (seg + half, seg))
     first_rows, tail_rows, second_rows = pl.ds(0, seg), pl.ds(seg, half), pl.ds(seg + half, seg)
     bases, parts, starts = layout
+    z_order = sorted(range(n_z - 1), key=lambda k: k + 1 != n_z // 2)
     z_bases = [sum(parts[:i]) for i in range(3)]
 
     loads = [
@@ -320,7 +321,7 @@
     def pair_finish(s):
         pair_copy(s).wait_recv()
         half_sum[region(s), :] = acc[core, region(s), :] + pair_recv[region(s), :]
-        for k in range(n_z - 1):
+        for k in z_order:
             z_copy(s, k).start()
 
     def z_finish(s):
@@ -336,7 +337,7 @@
         return total_of(total * total)
 
     def gather_start(s):
-        for k in range(n_z - 1):
+        for k in z_order:
             ag_copy(s, k, z).start()
 
     def gather_pass():

time: 86.9 us -> 86.2 us (level)
  no operation moved by 1% of the time
where the time goes in v6:
time: 86.2 us; the launch traced here: 86 us
  Pallas kernels  85.4 us (99%)
    pallas_call x1, Pallas kernels, per_device(): pl.pallas_call(functools.partial(kernel, n_mem, n_lat, seg, (bases, parts...  84.6 us

profile of v6, /device:TPU:0, one launch (start us, length us, event | category | flops | bytes accessed | tf_op | source)
XLA Modules:
  0.0 86.0 jit_solution(12328153608673269944)
XLA Ops:
  0.6 84.6 %shard_map.113 = (f32[6,32,320]{2,1,0:T(8,128)S(1)}, f32[3,24,160]{2,1,0:T(8,128)S(1)}) custom-call(bf16[32,3,24,1280]{3,2,1,0:T(8,128)(2,1)} %pert_hbm.1, f32[6,32,320]{2,1,0:T(8,128)} %bitcast.2, f32[3,24,1280]{2,1,0:T(8,128)} %innov_hbm.1, f32[3]{0:T(128)} %thr_hbm.1, bf16[3,192,144]{2,1,0:T(8,128)(2,1)} %constant.12.clone.rows_up_hbm, ...), custom_call_target="tpu_custom_call" | custom-call | tf_op jit(solution)/shard_map/pallas_call | solution.py:560
  85.3 0.7 shard_map.114

commit v7 on v6

--- a/solution.py
+++ b/solution.py
@@ -324,7 +324,7 @@
         for k in z_order:
             z_copy(s, k).start()
 
-    def z_finish(s):
+    def z_finish(s, early):
         for k in range(n_z - 1):
             z_copy(s, k).wait_recv()
         total = half_sum[part_rows(s, z), :]
@@ -332,7 +332,7 @@
             total = total + z_recv[k, pl.ds(z_bases[s], parts[s]), :]
         total = total * (1.0 / SCALE)
         image[core, part_rows(s, z), :] = total
-        if s < 2:
+        if s < early:
             gather_start(s)
         return total_of(total * total)
 
@@ -358,7 +358,7 @@
     def total_of(squares):
         return jnp.sum(squares.reshape(-1, 8, LANES), axis=0)
 
-    def forward_all():
+    def forward_all(early):
         acc[...] = jnp.zeros_like(acc)
         over_chunks(forward_first)
         pair_copy(0).start()
@@ -373,9 +373,9 @@
         pair_copy(2).start()
         pair_finish(1)
         pair_finish(2)
-        squares = z_finish(0)
-        squares = squares + z_finish(1)
-        squares = squares + z_finish(2)
+        squares = z_finish(0, early)
+        squares = squares + z_finish(1, early)
+        squares = squares + z_finish(2, early)
         return squares
 
     def sl_copy(it, k):
@@ -429,7 +429,7 @@
         return carry
 
     lax.fori_loop(0, pert.shape[0], widen, 0)
-    forward_all()
+    forward_all(2)
     gather_start(2)
     sent_all(g_copy)
     gather_pass()
@@ -463,11 +463,12 @@
 
         grad_sq = gradient(0)
         grad_sq = grad_sq + gradient(1)
-        image_sq = forward_all()
+        image_sq = forward_all(1)
         sums = jnp.concatenate([jnp.sum(grad_sq, axis=0, keepdims=True), jnp.sum(image_sq, axis=0, keepdims=True)], axis=0)
         mem_send[...] = sums
         for k in range(n_mem - 1):
             sm_copy(it, k).start()
+        gather_start(1)
         gather_start(2)
         sent_all(c_copy)
         sent_all(g_copy)

time: 86.2 us -> 86.1 us (level)
  no operation moved by 1% of the time
where the time goes in v7:
time: 86.1 us; the launch traced here: 85.9 us
  Pallas kernels  85.2 us (99%)
    pallas_call x1, Pallas kernels, per_device(): pl.pallas_call(functools.partial(kernel, n_mem, n_lat, seg, (bases, parts...  84.5 us

profile of v7, /device:TPU:0, one launch (start us, length us, event | category | flops | bytes accessed | tf_op | source)
XLA Modules:
  0.0 85.9 jit_solution(2616638247408624183)
XLA Ops:
  0.6 84.5 %shard_map.113 = (f32[6,32,320]{2,1,0:T(8,128)S(1)}, f32[3,24,160]{2,1,0:T(8,128)S(1)}) custom-call(bf16[32,3,24,1280]{3,2,1,0:T(8,128)(2,1)} %pert_hbm.1, f32[6,32,320]{2,1,0:T(8,128)} %bitcast.2, f32[3,24,1280]{2,1,0:T(8,128)} %innov_hbm.1, f32[3]{0:T(128)} %thr_hbm.1, bf16[3,192,144]{2,1,0:T(8,128)(2,1)} %constant.12.clone.rows_up_hbm, ...), custom_call_target="tpu_custom_call" | custom-call | tf_op jit(solution)/shard_map/pallas_call | solution.py:561
  85.1 0.7 shard_map.114
